TPU v7x, 32 devices: a whole 2x2x4 slice. The times are simulated.
32 devices in a mesh: angle: 8 (over z, y), tile: 2 (over x), half: 2 (over core).
Axes of the slice: x: 2, y: 2, z: 4, core: 2. Of those that a mesh axis runs over, the one named last changes fastest.
Arguments:
- projection: float32 [16, 2, 64, 256], P(('angle', 'half'), None, 'tile'), may hold values from -6 to 6
- multiplier: float32 [16, 2, 64, 256], P(('angle', 'half'), None, 'tile'), may hold values from -3 to 3
- reprojection: float32 [16, 64, 256], P(('angle', 'half'), 'tile'), may hold values from -6 to 6
- intensity: bfloat16 [16, 64, 64, 128], P(('angle', 'half'), 'tile'), may hold values from 0 to 4
- row_start: int32 [16, 64], P(('angle', 'half'), 'tile'), may hold values from -32 to 0
- column_start: int32 [16, 64], P(('angle', 'half'), 'tile'), may hold values from 0 to 128
- probe_field: float32 [2, 64, 128], replicated, may hold values from -6 to 6
- probe_mask: int32 [64, 128], replicated, may hold values 0 or 1
- weights: bfloat16 [16, 2, 4, 128, 512], P('angle'), may hold values from -0.125 to 0.125
- ray_blocks: int32 [16, 2, 4], P('angle'), may hold values from 0 to 127, as said below
- ray_counts: int32 [16, 2], P('angle'), may hold values from 1 to 4, as said below
- volume: float32 [128, 64, 512], P('angle', ('tile', 'half')), may hold values from -6 to 6
Outputs:
- updated_projection: float32 [16, 2, 64, 256], P(('angle', 'half'), None, 'tile')
- volume_new: float32 [128, 64, 512], P('angle', ('tile', 'half'))
- multiplier_new: float32 [16, 2, 64, 256], P('angle', None, ('tile', 'half'))
Inputs may be any that keep to these rules, and one draw needn't show every extreme that they name: A ray block uses its first ray_counts weight tiles; some ray block uses all 4. `ray_blocks`: slots at or past a ray block's count are not used. Split the angles into aligned groups of 2 and the pixel blocks into aligned groups of 16: the 16 slots of one angle group name blocks of one block group at most 2 times, and exactly 2 times for some block group.
All inputs are finite; a program needn't handle non-finite values.
Results may differ from a plain program's by a relative error of at most 0.008.
Values may be sent and summed in bfloat16 or wider, within the bound.
A program may use at most 64 MiB of HBM per device.

v0:
```python
import math

import jax
import jax.numpy as jnp
from jax import lax
from jax.sharding import PartitionSpec as P

PR = 64
PC = 128
NW = 256
PIX = 512
RB = 128
CMAX = 4
HALO = 32
NRB = 2


penalty = 0.5
descent = 0.25
volume_step = 1.0
damping = 0.1
highest = lax.Precision.HIGHEST


def extended_2(value, sides, width):
    for axis, dim in sides:
        devices, length = (lax.axis_size(axis), value.shape[dim])
        up = [(i, (i + 1) % devices) for i in range(devices - 1)]
        down = [(j, i) for i, j in up]
        last = lax.slice_in_dim(value, length - width, length, axis=dim)
        first = lax.slice_in_dim(value, 0, width, axis=dim)
        before = lax.ppermute(last, axis, up)
        after = lax.ppermute(first, axis, down)
        value = jnp.concatenate([before, value, after], axis=dim)
    return value


def tables(length):
    counter = lax.iota(jnp.int32, length)
    phase = (counter[:, None] * counter[None, :] % length).astype(jnp.float32) * (
        2.0 * math.pi / length
    )
    norming = 1.0 / math.sqrt(length)
    return (jnp.cos(phase) * norming, jnp.sin(phase) * norming)


def left_apply(matrix, values):
    return jnp.einsum("jk,bkl->bjl", matrix, values, precision=highest)


def right_apply(values, matrix):
    return jnp.einsum("bjl,lm->bjm", values, matrix, precision=highest)


def transform(real_part, imag_part, sign):
    row_cos, row_sin = tables(PR)
    col_cos, col_sin = tables(PC)
    first_real = left_apply(row_cos, real_part) - sign * left_apply(row_sin, imag_part)
    first_imag = left_apply(row_cos, imag_part) + sign * left_apply(row_sin, real_part)
    out_real = right_apply(first_real, col_cos) - sign * right_apply(first_imag, col_sin)
    out_imag = right_apply(first_imag, col_cos) + sign * right_apply(first_real, col_sin)
    return (out_real, out_imag)


def shards(
    projection,
    multiplier,
    reprojection,
    intensity,
    row_start,
    column_start,
    probe_field,
    probe_mask,
    weights,
    ray_blocks,
    ray_counts,
    volume,
):
    extended = extended_2(projection, (("tile", 2),), HALO)
    band_rows = projection.shape[2]
    ext_rows = extended.shape[2]
    angles_here, patches_here = row_start.shape
    masked_probe = probe_field * probe_mask.astype(jnp.float32)[None]
    first_rows = row_start + HALO
    zero_index = jnp.zeros((), jnp.int32)

    def cut_angle(source, rows_in, columns_in):

        def cutout(first_row, first_column):
            return lax.dynamic_slice(source, (zero_index, first_row, first_column), (2, PR, PC))

        return jax.vmap(cutout)(rows_in, columns_in)

    pieces = jax.vmap(cut_angle)(extended, first_rows, column_start)
    flat = pieces.reshape(angles_here * patches_here, 2, PR, PC)
    wave_real = masked_probe[0] * flat[:, 0] - masked_probe[1] * flat[:, 1]
    wave_imag = masked_probe[0] * flat[:, 1] + masked_probe[1] * flat[:, 0]
    far_real, far_imag = transform(wave_real, wave_imag, -1.0)
    measured = jnp.sqrt(intensity.astype(jnp.float32)).reshape(angles_here * patches_here, PR, PC)
    factor = 1.0 - measured / jnp.sqrt(far_real * far_real + far_imag * far_imag + 1.0)
    back_real, back_imag = transform(far_real * factor, far_imag * factor, 1.0)
    grad_real = masked_probe[0] * back_real + masked_probe[1] * back_imag
    grad_imag = masked_probe[0] * back_imag - masked_probe[1] * back_real
    patch_grads = jnp.stack([grad_real, grad_imag], axis=1).reshape(
        angles_here, patches_here, 2, PR, PC
    )
    row_pick = (
        lax.iota(jnp.int32, ext_rows)[None, None, None, :]
        == first_rows[:, :, None, None] + lax.iota(jnp.int32, PR)[None, None, :, None]
    ).astype(jnp.float32)
    column_pick = (
        lax.iota(jnp.int32, NW)[None, None, None, :]
        == column_start[:, :, None, None] + lax.iota(jnp.int32, PC)[None, None, :, None]
    ).astype(jnp.float32)
    sectioned = jnp.einsum("ajpq,ajcpl->ajcql", row_pick, patch_grads, precision=highest)
    summed = jnp.einsum("ajcql,ajlm->acqm", sectioned, column_pick, precision=highest)
    rims = jnp.concatenate([summed[:, :, :HALO], summed[:, :, ext_rows - HALO :]], axis=2)
    rim_rows = extended_2(rims, (("tile", 2),), HALO)
    gradient = summed[:, :, HALO : HALO + band_rows]
    gradient = gradient.at[:, :, :HALO].add(rim_rows[:, :, :HALO])
    gradient = gradient.at[:, :, band_rows - HALO :].add(rim_rows[:, :, 3 * HALO :])
    holder = jnp.stack([jnp.ones_like(reprojection), reprojection], axis=1)
    updated = projection - descent * (gradient + penalty * (projection - holder) + multiplier)
    bundle = jnp.concatenate([updated, multiplier], axis=1)
    moved = lax.all_to_all(bundle, "half", split_axis=2, concat_axis=0, tiled=True)
    target = moved[:, 1] + moved[:, 3] / penalty
    angle_count = weights.shape[0]
    slice_rows = volume.shape[1]
    own_blocks = volume.shape[0]
    live = lax.iota(jnp.int32, CMAX)[None, None, :] < ray_counts[:, :, None]
    groups = lax.axis_size("angle")
    slot_count = angle_count * NRB * CMAX
    capacity = max(2, -(-slot_count // groups))
    flat_ids = ray_blocks.reshape(slot_count)
    owners = flat_ids // own_blocks
    local_ids = flat_ids % own_blocks
    owner_hits = (owners[:, None] == lax.iota(jnp.int32, groups)[None, :]).astype(jnp.int32)
    slot_ranks = jnp.sum((jnp.cumsum(owner_hits, axis=0) - 1) * owner_hits, axis=1)
    slot_place = owners * capacity + slot_ranks
    requests = (
        jnp.zeros((groups * capacity,), jnp.int32)
        .at[slot_place]
        .set(local_ids)
        .reshape(groups, capacity)
    )
    wanted = lax.all_to_all(requests, "angle", split_axis=0, concat_axis=0, tiled=True).reshape(
        groups * capacity
    )
    live_half = live.astype(jnp.bfloat16)[:, :, :, None, None]

    def fetch_blocks(field):
        replies = field.astype(jnp.bfloat16)[wanted].reshape(groups, capacity, slice_rows, PIX)
        arrived = lax.all_to_all(replies, "angle", split_axis=0, concat_axis=0, tiled=True)
        picked = arrived.reshape(groups * capacity, slice_rows, PIX)[slot_place]
        picked = picked.reshape(angle_count, NRB, CMAX, slice_rows, PIX) * live_half
        result = jnp.einsum(
            "tkcrp,tkcsp->tskr", weights, picked, preferred_element_type=jnp.float32
        )
        return result.reshape(angle_count, slice_rows, NW)

    sinogram = fetch_blocks(volume)
    residual = (sinogram - target).astype(jnp.bfloat16).reshape(angle_count, slice_rows, NRB, RB)
    spread = (
        jnp.einsum("tkcrp,tskr->tkcsp", weights, residual, preferred_element_type=jnp.float32)
        * live.astype(jnp.float32)[:, :, :, None, None]
    )
    outgoing = (
        jnp.zeros((groups * capacity, slice_rows, PIX), jnp.float32)
        .at[slot_place]
        .set(spread.reshape(slot_count, slice_rows, PIX))
    )
    incoming = lax.all_to_all(
        outgoing.reshape(groups, capacity, slice_rows, PIX).astype(jnp.bfloat16),
        "angle",
        split_axis=0,
        concat_axis=0,
        tiled=True,
    ).astype(jnp.float32)
    placing = (wanted[:, None] == lax.iota(jnp.int32, own_blocks)[None, :]).astype(jnp.float32)
    block_grad = jnp.einsum(
        "nj,nsp->jsp",
        placing,
        incoming.reshape(groups * capacity, slice_rows, PIX),
        precision=highest,
    )
    new_volume = volume - volume_step * (block_grad + damping * volume)
    fresh = fetch_blocks(new_volume)
    fresh_holder = jnp.stack([jnp.ones_like(fresh), fresh], axis=1)
    new_multiplier = moved[:, 2:] + penalty * (moved[:, :2] - fresh_holder)
    return (updated, new_volume, new_multiplier)


def solution(mesh):
    return jax.shard_map(
        shards,
        mesh=mesh,
        in_specs=(
            P(("angle", "half"), None, "tile", None),
            P(("angle", "half"), None, "tile", None),
            P(("angle", "half"), "tile", None),
            P(("angle", "half"), "tile", None, None),
            P(("angle", "half"), "tile"),
            P(("angle", "half"), "tile"),
            P(),
            P(),
            P("angle", None, None, None, None),
            P("angle", None, None),
            P("angle", None),
            P("angle", ("tile", "half"), None),
        ),
        out_specs=(
            P(("angle", "half"), None, "tile", None),
            P("angle", ("tile", "half"), None),
            P("angle", None, ("tile", "half"), None),
        ),
        check_vma=False,
    )
```

profile of v0, /device:TPU:0, one launch (start us, length us, event | category | flops | bytes accessed | tf_op | source)
XLA Modules:
  0.0 196.7 jit_solution(8070560214326349281)
XLA Ops:
  0.6 5.0 %collective-permute-start = (f32[1,2,32,256]{3,2,1,0:T(8,128)}, f32[1,2,32,256]{3,2,1,0:T(8,128)S(1)}, u32[]{:S(2)}, u32[]{:S(2)}) collective-permute-start(f32[1,2,32,256]{3,2,1,0:T(8,128)} %param.20), channel_id=1, source_target_pairs={{0,2},{1,3},{4,6},{5,7},{8,10},{9,11},{12,14},{13,15},{16,18},{17,... | collective-permute-start | bytes 196616 | tf_op jit(solution)/shard_map/ppermute | solution.py:32
  10.1 5.8 %all-to-all-start = ((s32[8,1,2]{2,1,0:T(1,128)}), s32[8,1,2]{2,1,0:T(1,128)S(1)}, u32[]{:S(2)}, u32[]{:S(2)}) async-start(s32[8,1,2]{2,1,0:T(1,128)} %bitcast.32), calls=%async_computation | async-start | bytes 8192 | tf_op jit(solution)/shard_map/all_to_all | solution.py:146
  23.3 83.1 %while.5 = (s32[]{:T(128)}, f32[1,2,96,256]{3,2,1,0:T(8,128)S(1)}, s32[32,4]{0,1:T(4,128)S(1)}, f32[32,2,64,128]{3,2,0,1:T(8,128)}, s32[]{:T(128)}) while((s32[]{:T(128)}, f32[1,2,96,256]{3,2,1,0:T(8,128)S(1)}, s32[32,4]{0,1:T(4,128)S(1)}, f32[32,2,64,128]{3,2,0,1:T(8,128)}, s32[]{:T(128)}) %tuple.48), condition=%wide.while_cond.2, body=%wide.while_body.2.sunk | while | flops 2 | bytes 132721 | solution.py:90
  23.9 2.0 %bitcast_dynamic-update-slice_fusion.2 = f32[32,2,64,128]{3,2,0,1:T(8,128)} fusion(f32[32,2,64,128]{3,2,0,1:T(8,128)} %get-tuple-element.124, s32[]{:T(128)} %get-tuple-element.121, f32[1,2,96,256]{3,2,1,0:T(8,128)S(1)} %get-tuple-element.127, s32[]{:T(128)} %bitcast.203, s32[]{:T(128)} %bitcast.204), kind=kLoop, calls=%fused_computation.6.clone.1 | loop fusion | bytes 132608 | tf_op jit(solution)/shard_map/vmap(vmap())/gather
  42.1 2.0 %bitcast_dynamic-update-slice_fusion.2 = f32[32,2,64,128]{3,2,0,1:T(8,128)} fusion(f32[32,2,64,128]{3,2,0,1:T(8,128)} %get-tuple-element.124, s32[]{:T(128)} %get-tuple-element.121, f32[1,2,96,256]{3,2,1,0:T(8,128)S(1)} %get-tuple-element.127, s32[]{:T(128)} %bitcast.203, s32[]{:T(128)} %bitcast.204), kind=kLoop, calls=%fused_computation.6.clone.1 | loop fusion | bytes 132608 | tf_op jit(solution)/shard_map/vmap(vmap())/gather
  49.9 2.0 %bitcast_dynamic-update-slice_fusion.2 = f32[32,2,64,128]{3,2,0,1:T(8,128)} fusion(f32[32,2,64,128]{3,2,0,1:T(8,128)} %get-tuple-element.124, s32[]{:T(128)} %get-tuple-element.121, f32[1,2,96,256]{3,2,1,0:T(8,128)S(1)} %get-tuple-element.127, s32[]{:T(128)} %bitcast.203, s32[]{:T(128)} %bitcast.204), kind=kLoop, calls=%fused_computation.6.clone.1 | loop fusion | bytes 132608 | tf_op jit(solution)/shard_map/vmap(vmap())/gather
  70.7 2.0 %bitcast_dynamic-update-slice_fusion.2 = f32[32,2,64,128]{3,2,0,1:T(8,128)} fusion(f32[32,2,64,128]{3,2,0,1:T(8,128)} %get-tuple-element.124, s32[]{:T(128)} %get-tuple-element.121, f32[1,2,96,256]{3,2,1,0:T(8,128)S(1)} %get-tuple-element.127, s32[]{:T(128)} %bitcast.203, s32[]{:T(128)} %bitcast.204), kind=kLoop, calls=%fused_computation.6.clone.1 | loop fusion | bytes 132608 | tf_op jit(solution)/shard_map/vmap(vmap())/gather
  78.5 2.0 %bitcast_dynamic-update-slice_fusion.2 = f32[32,2,64,128]{3,2,0,1:T(8,128)} fusion(f32[32,2,64,128]{3,2,0,1:T(8,128)} %get-tuple-element.124, s32[]{:T(128)} %get-tuple-element.121, f32[1,2,96,256]{3,2,1,0:T(8,128)S(1)} %get-tuple-element.127, s32[]{:T(128)} %bitcast.203, s32[]{:T(128)} %bitcast.204), kind=kLoop, calls=%fused_computation.6.clone.1 | loop fusion | bytes 132608 | tf_op jit(solution)/shard_map/vmap(vmap())/gather
  81.1 2.0 %bitcast_dynamic-update-slice_fusion.2 = f32[32,2,64,128]{3,2,0,1:T(8,128)} fusion(f32[32,2,64,128]{3,2,0,1:T(8,128)} %get-tuple-element.124, s32[]{:T(128)} %get-tuple-element.121, f32[1,2,96,256]{3,2,1,0:T(8,128)S(1)} %get-tuple-element.127, s32[]{:T(128)} %bitcast.203, s32[]{:T(128)} %bitcast.204), kind=kLoop, calls=%fused_computation.6.clone.1 | loop fusion | bytes 132608 | tf_op jit(solution)/shard_map/vmap(vmap())/gather
  91.5 2.0 %bitcast_dynamic-update-slice_fusion.2 = f32[32,2,64,128]{3,2,0,1:T(8,128)} fusion(f32[32,2,64,128]{3,2,0,1:T(8,128)} %get-tuple-element.124, s32[]{:T(128)} %get-tuple-element.121, f32[1,2,96,256]{3,2,1,0:T(8,128)S(1)} %get-tuple-element.127, s32[]{:T(128)} %bitcast.203, s32[]{:T(128)} %bitcast.204), kind=kLoop, calls=%fused_computation.6.clone.1 | loop fusion | bytes 132608 | tf_op jit(solution)/shard_map/vmap(vmap())/gather
  96.7 2.0 %bitcast_dynamic-update-slice_fusion.2 = f32[32,2,64,128]{3,2,0,1:T(8,128)} fusion(f32[32,2,64,128]{3,2,0,1:T(8,128)} %get-tuple-element.124, s32[]{:T(128)} %get-tuple-element.121, f32[1,2,96,256]{3,2,1,0:T(8,128)S(1)} %get-tuple-element.127, s32[]{:T(128)} %bitcast.203, s32[]{:T(128)} %bitcast.204), kind=kLoop, calls=%fused_computation.6.clone.1 | loop fusion | bytes 132608 | tf_op jit(solution)/shard_map/vmap(vmap())/gather
  101.9 2.0 %bitcast_dynamic-update-slice_fusion.2 = f32[32,2,64,128]{3,2,0,1:T(8,128)} fusion(f32[32,2,64,128]{3,2,0,1:T(8,128)} %get-tuple-element.124, s32[]{:T(128)} %get-tuple-element.121, f32[1,2,96,256]{3,2,1,0:T(8,128)S(1)} %get-tuple-element.127, s32[]{:T(128)} %bitcast.203, s32[]{:T(128)} %bitcast.204), kind=kLoop, calls=%fused_computation.6.clone.1 | loop fusion | bytes 132608 | tf_op jit(solution)/shard_map/vmap(vmap())/gather
  106.5 3.0 %fusion.39 = f32[32,128,64]{1,2,0:T(8,128)S(1)} fusion(f32[32,2,64,128]{3,2,0,1:T(8,128)} %get-tuple-element.50, f32[64,128]{1,0:T(8,128)S(1)} %get-tuple-element.78, f32[64,128]{1,0:T(8,128)S(1)} %get-tuple-element.77), kind=kOutput, calls=%fused_computation.61 | convolution fusion | flops 202174464 | bytes 3211264 | tf_op jit(solution)/shard_map/jk,bkl->bjl/dot_general | solution.py:48
  130.8 2.4 %fusion.4 = f32[32,2,128,96]{2,3,1,0:T(8,128)S(1)} fusion(s32[32,64]{1,0:T(8,128)S(1)} %iota_add_fusion.1, f32[32,1,64,128]{3,2,0,1:T(8,128)S(1)} %get-tuple-element.74, f32[32,1,64,128]{3,2,0,1:T(8,128)S(1)} %get-tuple-element.73), kind=kOutput, calls=%fused_computation.13 | convolution fusion | flops 604700672 | bytes 5251072 | tf_op jit(solution)/shard_map/ajpq,ajcpl->ajcql/dot_general | solution.py:115
  133.2 2.2 %fusion.16 = f32[1,2,96,256]{3,2,1,0:T(8,128)S(1)} fusion(s32[32,128]{1,0:T(8,128)S(1)} %iota_add_fusion, f32[32,2,128,96]{2,3,1,0:T(8,128)S(1)} %fusion.4), kind=kOutput, calls=%fused_computation.35 | convolution fusion | flops 2416967680 | bytes 3358720 | tf_op jit(solution)/shard_map/ajcql,ajlm->acqm/dot_general | solution.py:116
  135.4 4.5 %collective-permute-start.2 = (f32[1,2,32,256]{3,2,1,0:T(8,128)S(1)}, f32[1,2,32,256]{3,2,1,0:T(8,128)S(1)}, u32[]{:S(2)}, u32[]{:S(2)}) collective-permute-start(f32[1,2,32,256]{3,2,1,0:T(8,128)S(1)} %get-tuple-element.75), channel_id=1, source_target_pairs={{0,2},{1,3},{4,6},{5,7},{8,10},{9,11},{12,14},{13,15},{16,18},{17,... | collective-permute-start | bytes 196616 | tf_op jit(solution)/shard_map/ppermute | solution.py:32
  142.6 3.6 %collective-permute-done.3 = f32[1,2,32,256]{3,2,1,0:T(8,128)S(1)} collective-permute-done((f32[1,2,32,256]{3,2,1,0:T(8,128)S(1)}, f32[1,2,32,256]{3,2,1,0:T(8,128)S(1)}, u32[]{:S(2)}, u32[]{:S(2)}) %collective-permute-start.3) | collective-permute-done | bytes 65568 | tf_op jit(solution)/shard_map/ppermute | solution.py:33
  146.9 3.8 %all_to_all.42 = f32[1,4,32,256]{3,1,0,2:T(4,128)S(1)} all-to-all(f32[1,4,32,256]{3,1,0,2:T(4,128)S(1)} %copy.54), channel_id=1, replica_groups=mesh['angle'=8,'tile'=2,'half'=2] {'half'}, dimensions={2} | all-to-all | bytes 262144 | tf_op jit(solution)/shard_map/all_to_all | solution.py:125
  150.8 4.5 %all-to-all-start.1 = ((bf16[8,2,16,512]{3,2,1,0:T(8,128)(2,1)}), bf16[8,2,16,512]{3,2,1,0:T(8,128)(2,1)S(1)}, u32[]{:S(2)}, u32[]{:S(2)}) async-start(bf16[8,2,16,512]{3,2,1,0:T(8,128)(2,1)} %bitcast.35), calls=%async_computation.1 | async-start | bytes 524288 | tf_op jit(solution)/shard_map/all_to_all | solution.py:153
  155.5 9.1 %all-to-all-done.1 = bf16[8,2,16,512]{3,2,1,0:T(8,128)(2,1)S(1)} async-done(((bf16[8,2,16,512]{3,2,1,0:T(8,128)(2,1)}), bf16[8,2,16,512]{3,2,1,0:T(8,128)(2,1)S(1)}, u32[]{:S(2)}, u32[]{:S(2)}) %all-to-all-start.1) | async-done | bytes 262176 | tf_op jit(solution)/shard_map/all_to_all | solution.py:153
  168.2 3.6 %all-to-all-start.3 = ((bf16[8,2,16,512]{3,1,2,0:T(2,128)(2,1)}), bf16[8,2,16,512]{3,1,2,0:T(2,128)(2,1)S(1)}, u32[]{:S(2)}, u32[]{:S(2)}) async-start(bf16[8,2,16,512]{3,1,2,0:T(2,128)(2,1)} %copy.57), calls=%async_computation.3 | async-start | bytes 524288 | tf_op jit(solution)/shard_map/all_to_all | solution.py:172
  173.1 7.3 %all-to-all-done.3 = bf16[8,2,16,512]{3,1,2,0:T(2,128)(2,1)S(1)} async-done(((bf16[8,2,16,512]{3,1,2,0:T(2,128)(2,1)}), bf16[8,2,16,512]{3,1,2,0:T(2,128)(2,1)S(1)}, u32[]{:S(2)}, u32[]{:S(2)}) %all-to-all-start.3) | async-done | bytes 262176 | tf_op jit(solution)/shard_map/all_to_all | solution.py:172
  182.6 3.6 %all-to-all-start.4 = ((bf16[8,2,16,512]{3,2,1,0:T(8,128)(2,1)}), bf16[8,2,16,512]{3,2,1,0:T(8,128)(2,1)S(1)}, u32[]{:S(2)}, u32[]{:S(2)}) async-start(bf16[8,2,16,512]{3,2,1,0:T(8,128)(2,1)} %bitcast.51), calls=%async_computation.4 | async-start | bytes 524288 | tf_op jit(solution)/shard_map/all_to_all | solution.py:153
  187.3 7.4 %all-to-all-done.4 = bf16[8,2,16,512]{3,2,1,0:T(8,128)(2,1)S(1)} async-done(((bf16[8,2,16,512]{3,2,1,0:T(8,128)(2,1)}), bf16[8,2,16,512]{3,2,1,0:T(8,128)(2,1)S(1)}, u32[]{:S(2)}, u32[]{:S(2)}) %all-to-all-start.4) | async-done | bytes 262176 | tf_op jit(solution)/shard_map/all_to_all | solution.py:153
  (182 shorter events, 111.5 us)
Async XLA Ops:
  0.6 164.5 %copy-start = (bf16[2,2,4,128,512]{4,3,2,1,0:T(8,128)(2,1)S(1)}, bf16[2,2,4,128,512]{4,3,2,1,0:T(8,128)(2,1)}, u32[]{:S(2)}) copy-start(bf16[2,2,4,128,512]{4,3,2,1,0:T(8,128)(2,1)} %param.28) | copy-start | bytes 6291460
  0.6 21.8 %collective-permute-start = (f32[1,2,32,256]{3,2,1,0:T(8,128)}, f32[1,2,32,256]{3,2,1,0:T(8,128)S(1)}, u32[]{:S(2)}, u32[]{:S(2)}) collective-permute-start(f32[1,2,32,256]{3,2,1,0:T(8,128)} %param.20), channel_id=1, source_target_pairs={{0,2},{1,3},{4,6},{5,7},{8,10},{9,11},{12,14},{13,15},{16,18},{17,... | collective-permute-start | bytes 196616 | tf_op jit(solution)/shard_map/ppermute | solution.py:32
  5.7 16.8 %collective-permute-start.1 = (f32[1,2,32,256]{3,2,1,0:T(8,128)}, f32[1,2,32,256]{3,2,1,0:T(8,128)S(1)}, u32[]{:S(2)}, u32[]{:S(2)}) collective-permute-start(f32[1,2,32,256]{3,2,1,0:T(8,128)} %param.20), channel_id=1, source_target_pairs={{2,0},{3,1},{6,4},{7,5},{10,8},{11,9},{14,12},{15,13},{18,16},{19,... | collective-permute-start | bytes 196616 | tf_op jit(solution)/shard_map/ppermute | solution.py:33
  10.1 12.3 %all-to-all-start = ((s32[8,1,2]{2,1,0:T(1,128)}), s32[8,1,2]{2,1,0:T(1,128)S(1)}, u32[]{:S(2)}, u32[]{:S(2)}) async-start(s32[8,1,2]{2,1,0:T(1,128)} %bitcast.32), calls=%async_computation | async-start | bytes 8192 | tf_op jit(solution)/shard_map/all_to_all | solution.py:146
  106.5 3.0 %copy-start.2 = (f32[32,2,64,128]{3,2,0,1:T(8,128)S(1)}, f32[32,2,64,128]{3,2,0,1:T(8,128)}, u32[]{:S(2)}) copy-start(f32[32,2,64,128]{3,2,0,1:T(8,128)} %get-tuple-element.50) | copy-start | bytes 6291460
  117.2 1.2 copy-start.1
  133.2 13.0 %copy-start.4 = (f32[1,2,32,256]{3,2,1,0:T(8,128)S(1)}, f32[1,2,32,256]{3,2,1,0:T(8,128)}, u32[]{:S(2)}) copy-start(f32[1,2,32,256]{3,2,1,0:T(8,128)} %param.20) | copy-start | bytes 196612
  133.2 13.0 %copy-start.5 = (f32[1,2,32,256]{3,2,1,0:T(8,128)S(1)}, f32[1,2,32,256]{3,2,1,0:T(8,128)}, u32[]{:S(2)}) copy-start(f32[1,2,32,256]{3,2,1,0:T(8,128)} %param.21) | copy-start | bytes 196612
  133.2 13.0 %copy-start.7 = (f32[1,32,256]{2,1,0:T(8,128)S(1)}, f32[1,32,256]{2,1,0:T(8,128)}, u32[]{:S(2)}) copy-start(f32[1,32,256]{2,1,0:T(8,128)} %param.22) | copy-start | bytes 98308
  135.4 19.9 %copy-start.8 = (s32[2,2]{1,0:T(2,128)S(1)}, s32[2,2]{1,0:T(2,128)}, u32[]{:S(2)}) copy-start(s32[2,2]{1,0:T(2,128)} %param.30) | copy-start | bytes 52
  135.4 7.1 %collective-permute-start.2 = (f32[1,2,32,256]{3,2,1,0:T(8,128)S(1)}, f32[1,2,32,256]{3,2,1,0:T(8,128)S(1)}, u32[]{:S(2)}, u32[]{:S(2)}) collective-permute-start(f32[1,2,32,256]{3,2,1,0:T(8,128)S(1)} %get-tuple-element.75), channel_id=1, source_target_pairs={{0,2},{1,3},{4,6},{5,7},{8,10},{9,11},{12,14},{13,15},{16,18},{17,... | collective-permute-start | bytes 196616 | tf_op jit(solution)/shard_map/ppermute | solution.py:32
  140.0 6.2 %collective-permute-start.3 = (f32[1,2,32,256]{3,2,1,0:T(8,128)S(1)}, f32[1,2,32,256]{3,2,1,0:T(8,128)S(1)}, u32[]{:S(2)}, u32[]{:S(2)}) collective-permute-start(f32[1,2,32,256]{3,2,1,0:T(8,128)S(1)} %get-tuple-element.76), channel_id=1, source_target_pairs={{2,0},{3,1},{6,4},{7,5},{10,8},{11,9},{14,12},{15,13},{18,16},{19,... | collective-permute-start | bytes 196616 | tf_op jit(solution)/shard_map/ppermute | solution.py:33
  146.2 0.6 copy-start.6
  150.8 13.7 %all-to-all-start.1 = ((bf16[8,2,16,512]{3,2,1,0:T(8,128)(2,1)}), bf16[8,2,16,512]{3,2,1,0:T(8,128)(2,1)S(1)}, u32[]{:S(2)}, u32[]{:S(2)}) async-start(bf16[8,2,16,512]{3,2,1,0:T(8,128)(2,1)} %bitcast.35), calls=%async_computation.1 | async-start | bytes 524288 | tf_op jit(solution)/shard_map/all_to_all | solution.py:153
  167.2 13.5 %copy-start.3 = (f32[16,16,512]{2,1,0:T(8,128)S(1)}, f32[16,16,512]{2,1,0:T(8,128)}, u32[]{:S(2)}) copy-start(f32[16,16,512]{2,1,0:T(8,128)} %param.31) | copy-start | bytes 1572868
  168.2 12.2 %all-to-all-start.3 = ((bf16[8,2,16,512]{3,1,2,0:T(2,128)(2,1)}), bf16[8,2,16,512]{3,1,2,0:T(2,128)(2,1)S(1)}, u32[]{:S(2)}, u32[]{:S(2)}) async-start(bf16[8,2,16,512]{3,1,2,0:T(2,128)(2,1)} %copy.57), calls=%async_computation.3 | async-start | bytes 524288 | tf_op jit(solution)/shard_map/all_to_all | solution.py:172
  182.6 12.1 %all-to-all-start.4 = ((bf16[8,2,16,512]{3,2,1,0:T(8,128)(2,1)}), bf16[8,2,16,512]{3,2,1,0:T(8,128)(2,1)S(1)}, u32[]{:S(2)}, u32[]{:S(2)}) async-start(bf16[8,2,16,512]{3,2,1,0:T(8,128)(2,1)} %bitcast.51), calls=%async_computation.4 | async-start | bytes 524288 | tf_op jit(solution)/shard_map/all_to_all | solution.py:153
where the time goes:
time: 198 us; the launch traced here: 197 us
  local copies, waits for them, and re-layouts  95.4 us (48%)
  matrix products  30.8 us (16%)
  starting transfers between devices  29.7 us (15%)
  waiting for transfers between devices  28.9 us (15%)
  other arithmetic  6.9 us (3%)
  blocking collectives  3.84 us (2%)
    gather x96, local copies, waits for them, and re-layouts  83.1 us
    all_to_all x2, waiting for transfers between devices, fetch_blocks(): lax.all_to_all(replies, 'angle', split_axis=0, concat_axis=0, tiled=True)  16.5 us
    dot_general x8, matrix products, left_apply(): return jnp.einsum('jk,bkl->bjl', matrix, values, precision=highest)  14.2 us
    dot_general x8, matrix products, right_apply(): return jnp.einsum('bjl,lm->bjm', values, matrix, precision=highest)  9.95 us
    ppermute x2, starting transfers between devices, extended_2(): before = lax.ppermute(last, axis, up)  9.56 us
    all_to_all x2, starting transfers between devices, fetch_blocks(): lax.all_to_all(replies, 'angle', split_axis=0, concat_axis=0, tiled=True)  8.09 us
    all_to_all x1, waiting for transfers between devices, shards(): lax.all_to_all(outgoing.reshape(groups, capacity, slice_rows, PIX).astype...  7.31 us
    all_to_all x1, starting transfers between devices, shards(): lax.all_to_all(requests, 'angle', split_axis=0, concat_axis=0, tiled=True)  5.83 us
  transfers between devices with their start and end apart: 8, of which 5 were waited for; matrix products, arithmetic and copies ran while one was open for 6% of the time, Pallas kernels for 0%

commit v1 on v0

v1 whole, which is shorter than its diff:
```python
import jax
import jax.numpy as jnp
import numpy as np
from jax import lax
from jax.experimental import pallas as pl
from jax.experimental.pallas import tpu as pltpu
from jax.sharding import PartitionSpec as P

PR = 64
PC = 128
NW = 256
PIX = 512
RB = 128
CMAX = 4
HALO = 32
NRB = 2


penalty = 0.5
descent = 0.25
volume_step = 1.0
damping = 0.1
highest = lax.Precision.HIGHEST


def neighbours(axis):
    devices = lax.axis_size(axis)
    up = [(i, i + 1) for i in range(devices - 1)]
    return up, [(j, i) for i, j in up]


def dft_blocks(sign):
    def table(length):
        counter = np.arange(length)
        phase = (counter[:, None] * counter[None, :] % length) * (2.0 * np.pi / length)
        return np.cos(phase) / np.sqrt(length), sign * np.sin(phase) / np.sqrt(length)

    row_cos, row_sin = table(PR)
    col_cos, col_sin = table(PC)
    left = np.block([[row_cos, -row_sin], [row_sin, row_cos]])
    right = np.block([[col_cos, col_sin], [-col_sin, col_cos]])
    return left.astype(np.float32), right.astype(np.float32)


CHUNK = 4


def ptycho_kernel(
    rows_ref, cols_ref, before_ref, own_ref, after_ref, measured_ref, field_ref, mask_ref,
    left_f_ref, right_f_ref, left_b_ref, right_b_ref,
    top_ref, mid_ref, bottom_ref, ext_ref, acc_ref, wave_ref,
):
    band = own_ref.shape[2]
    lanes = [slice(0, PC), slice(PC, NW)]
    for side in range(2):
        ext_ref[:, side, :HALO] = before_ref[0, :, :, lanes[side]]
        ext_ref[:, side, HALO : HALO + band] = own_ref[0, :, :, lanes[side]]
        ext_ref[:, side, HALO + band :] = after_ref[0, :, :, lanes[side]]
    acc_ref[...] = jnp.zeros_like(acc_ref)
    half = jnp.bfloat16
    mask = mask_ref[...].astype(jnp.float32)
    wave_ref[0] = field_ref[0] * mask
    wave_ref[1] = field_ref[1] * mask

    lane = lax.broadcasted_iota(jnp.int32, (PR, PC), 1)

    def dot(a, b):
        return jnp.dot(a, b, preferred_element_type=jnp.float32)

    def step(chunk, carry):
        waves = []
        places = []
        for j in range(CHUNK):
            p = chunk * CHUNK + j
            row = rows_ref[0, p] + HALO
            col = cols_ref[0, p]
            places.append((row, col))
            back_shift = lax.rem(NW - col, PC)

            def window(channel):
                near = pltpu.roll(ext_ref[channel, 0, pl.ds(row, PR), :], back_shift, 1)
                next_ = pltpu.roll(ext_ref[channel, 1, pl.ds(row, PR), :], back_shift, 1)
                return jnp.where(lane + col < PC, near, next_)

            o_re = window(0)
            o_im = window(1)
            p_re, p_im = wave_ref[0], wave_ref[1]
            waves.append(
                jnp.concatenate([p_re * o_re - p_im * o_im, p_re * o_im + p_im * o_re], axis=0)
            )
        wide = jnp.concatenate(waves, axis=1).astype(half)
        first = dot(left_f_ref[...], wide).astype(half)
        tall = jnp.concatenate(
            [
                jnp.concatenate(
                    [first[:PR, j * PC : (j + 1) * PC], first[PR:, j * PC : (j + 1) * PC]], axis=1
                )
                for j in range(CHUNK)
            ],
            axis=0,
        )
        far = dot(tall, right_f_ref[...])
        f_re, f_im = far[:, :PC], far[:, PC:]
        measured = measured_ref[0, pl.ds(chunk * CHUNK, CHUNK)].astype(jnp.float32)
        measured = measured.reshape(CHUNK * PR, PC)
        factor = 1.0 - jnp.sqrt(measured) * lax.rsqrt(f_re * f_re + f_im * f_im + 1.0)
        scaled = jnp.concatenate([f_re * factor, f_im * factor], axis=1).astype(half)
        second = dot(scaled, right_b_ref[...]).astype(half)
        wide = jnp.concatenate(
            [
                jnp.concatenate(
                    [second[j * PR : (j + 1) * PR, :PC], second[j * PR : (j + 1) * PR, PC:]], axis=0
                )
                for j in range(CHUNK)
            ],
            axis=1,
        )
        back = dot(left_b_ref[...], wide)
        for j in range(CHUNK):
            row, col = places[j]
            b_re = back[:PR, j * PC : (j + 1) * PC]
            b_im = back[PR:, j * PC : (j + 1) * PC]
            p_re, p_im = wave_ref[0], wave_ref[1]
            shift = lax.rem(col, PC)
            for channel, values in ((0, p_re * b_re + p_im * b_im), (1, p_re * b_im - p_im * b_re)):
                values = pltpu.roll(values, shift, 1)
                acc_ref[channel, 0, pl.ds(row, PR), :] += jnp.where(lane >= col, values, 0.0)
                acc_ref[channel, 1, pl.ds(row, PR), :] += jnp.where(lane >= col, 0.0, values)
        return carry

    lax.fori_loop(0, rows_ref.shape[1] // CHUNK, step, 0)
    for side in range(2):
        top_ref[0, :, :, lanes[side]] = acc_ref[:, side, :HALO]
        mid_ref[0, :, :, lanes[side]] = acc_ref[:, side, HALO : HALO + band]
        bottom_ref[0, :, :, lanes[side]] = acc_ref[:, side, HALO + band :]


def patch_sums(before, own, after, rows, cols, measured, field, mask):
    band = own.shape[2]
    left_f, right_f = dft_blocks(-1.0)
    left_b, right_b = dft_blocks(1.0)
    tables = [jnp.asarray(m, jnp.bfloat16) for m in (left_f, right_f, left_b, right_b)]
    vmem = pl.BlockSpec(memory_space=pltpu.VMEM)
    smem = pl.BlockSpec(memory_space=pltpu.SMEM)
    rim = jax.ShapeDtypeStruct(before.shape, jnp.float32)
    ext_rows = band + 2 * HALO
    return pl.pallas_call(
        ptycho_kernel,
        out_shape=(rim, jax.ShapeDtypeStruct(own.shape, jnp.float32), rim),
        in_specs=[smem, smem] + [vmem] * 10,
        out_specs=(vmem, vmem, vmem),
        scratch_shapes=[
            pltpu.VMEM((2, NW // PC, ext_rows, PC), jnp.float32),
            pltpu.VMEM((2, NW // PC, ext_rows, PC), jnp.float32),
            pltpu.VMEM((2, PR, PC), jnp.float32),
        ],
        cost_estimate=pl.CostEstimate(
            flops=2000000000, bytes_accessed=2000000, transcendentals=500000
        ),
    )(rows, cols, before, own, after, measured, field, mask, *tables)


def swap_half(value):
    return lax.ppermute(value, "half", [(0, 1), (1, 0)])


def to_slices(value):
    side = lax.axis_index("half")
    rows = value.shape[2] // 2
    low, high = value[:, :, :rows], value[:, :, rows:]
    kept = jnp.where(side == 0, low, high)
    other = swap_half(jnp.where(side == 0, high, low))
    return jnp.concatenate(
        [jnp.where(side == 0, kept, other), jnp.where(side == 0, other, kept)], axis=0
    )


def shards(
    projection,
    multiplier,
    reprojection,
    intensity,
    row_start,
    column_start,
    probe_field,
    probe_mask,
    weights,
    ray_blocks,
    ray_counts,
    volume,
):
    up, down = neighbours("tile")
    band_rows = projection.shape[2]
    before = lax.ppermute(projection[:, :, band_rows - HALO :], "tile", up)
    after = lax.ppermute(projection[:, :, :HALO], "tile", down)
    moved_mult = to_slices(multiplier)
    top, gradient, bottom = patch_sums(
        before, projection, after, row_start, column_start, intensity, probe_field, probe_mask
    )
    from_above = lax.ppermute(bottom, "tile", up)
    from_below = lax.ppermute(top, "tile", down)
    if band_rows == HALO:
        gradient = gradient + from_above + from_below
    else:
        gradient = gradient.at[:, :, :HALO].add(from_above)
        gradient = gradient.at[:, :, band_rows - HALO :].add(from_below)
    holder = jnp.stack([jnp.ones_like(reprojection), reprojection], axis=1)
    updated = projection - descent * (gradient + penalty * (projection - holder) + multiplier)
    moved = jnp.concatenate([to_slices(updated), moved_mult], axis=1)
    target = moved[:, 1] + moved[:, 3] / penalty
    angle_count = weights.shape[0]
    slice_rows = volume.shape[1]
    own_blocks = volume.shape[0]
    live = lax.iota(jnp.int32, CMAX)[None, None, :] < ray_counts[:, :, None]
    groups = lax.axis_size("angle")
    slot_count = angle_count * NRB * CMAX
    capacity = max(2, -(-slot_count // groups))
    flat_ids = ray_blocks.reshape(slot_count)
    owners = flat_ids // own_blocks
    local_ids = flat_ids % own_blocks
    owner_hits = (owners[:, None] == lax.iota(jnp.int32, groups)[None, :]).astype(jnp.int32)
    slot_ranks = jnp.sum((jnp.cumsum(owner_hits, axis=0) - 1) * owner_hits, axis=1)
    slot_place = owners * capacity + slot_ranks
    requests = (
        jnp.zeros((groups * capacity,), jnp.int32)
        .at[slot_place]
        .set(local_ids)
        .reshape(groups, capacity)
    )
    wanted = lax.all_to_all(requests, "angle", split_axis=0, concat_axis=0, tiled=True).reshape(
        groups * capacity
    )
    live_half = live.astype(jnp.bfloat16)[:, :, :, None, None]

    def fetch_blocks(field):
        replies = field.astype(jnp.bfloat16)[wanted].reshape(groups, capacity, slice_rows, PIX)
        arrived = lax.all_to_all(replies, "angle", split_axis=0, concat_axis=0, tiled=True)
        picked = arrived.reshape(groups * capacity, slice_rows, PIX)[slot_place]
        picked = picked.reshape(angle_count, NRB, CMAX, slice_rows, PIX) * live_half
        result = jnp.einsum(
            "tkcrp,tkcsp->tskr", weights, picked, preferred_element_type=jnp.float32
        )
        return result.reshape(angle_count, slice_rows, NW)

    sinogram = fetch_blocks(volume)
    residual = (sinogram - target).astype(jnp.bfloat16).reshape(angle_count, slice_rows, NRB, RB)
    spread = (
        jnp.einsum("tkcrp,tskr->tkcsp", weights, residual, preferred_element_type=jnp.float32)
        * live.astype(jnp.float32)[:, :, :, None, None]
    )
    outgoing = (
        jnp.zeros((groups * capacity, slice_rows, PIX), jnp.float32)
        .at[slot_place]
        .set(spread.reshape(slot_count, slice_rows, PIX))
    )
    incoming = lax.all_to_all(
        outgoing.reshape(groups, capacity, slice_rows, PIX).astype(jnp.bfloat16),
        "angle",
        split_axis=0,
        concat_axis=0,
        tiled=True,
    ).astype(jnp.float32)
    placing = (wanted[:, None] == lax.iota(jnp.int32, own_blocks)[None, :]).astype(jnp.float32)
    block_grad = jnp.einsum(
        "nj,nsp->jsp",
        placing,
        incoming.reshape(groups * capacity, slice_rows, PIX),
        precision=highest,
    )
    new_volume = volume - volume_step * (block_grad + damping * volume)
    fresh = fetch_blocks(new_volume)
    fresh_holder = jnp.stack([jnp.ones_like(fresh), fresh], axis=1)
    new_multiplier = moved[:, 2:] + penalty * (moved[:, :2] - fresh_holder)
    return (updated, new_volume, new_multiplier)


def solution(mesh):
    return jax.shard_map(
        shards,
        mesh=mesh,
        in_specs=(
            P(("angle", "half"), None, "tile", None),
            P(("angle", "half"), None, "tile", None),
            P(("angle", "half"), "tile", None),
            P(("angle", "half"), "tile", None, None),
            P(("angle", "half"), "tile"),
            P(("angle", "half"), "tile"),
            P(),
            P(),
            P("angle", None, None, None, None),
            P("angle", None, None),
            P("angle", None),
            P("angle", ("tile", "half"), None),
        ),
        out_specs=(
            P(("angle", "half"), None, "tile", None),
            P("angle", ("tile", "half"), None),
            P("angle", None, ("tile", "half"), None),
        ),
        check_vma=False,
    )
```

time: 198 us -> 82.6 us (0.42)
  local copies, waits for them, and re-layouts: 95.4 us -> 12.3 us
  matrix products: 30.8 us -> 2.05 us
  Pallas kernels: 0 us -> 9.08 us
  blocking collectives: 3.84 us -> 0 us
  starting transfers between devices: 29.7 us -> 26.4 us
  waiting for transfers between devices: 28.9 us -> 25.7 us
    gather x97 -> x0, local copies, waits for them, and re-layouts: 83.1 us -> none
    dot_general x18 -> x0, matrix products: 28.7 us -> none  [the longest x8 14.2 us: left_apply(): return jnp.einsum('jk,bkl->bjl', matrix, values, precision=highest)]
    pallas_call x0 -> x1, Pallas kernels: none -> 9.08 us  [patch_sums(): pl.pallas_call(ptycho_kernel, out_shape=(rim, jax.ShapeDtypeStruct(own.sh...]
    all_to_all x1 -> x0, blocking collectives: 3.84 us -> none  [shards(): lax.all_to_all(bundle, 'half', split_axis=2, concat_axis=0, tiled=True)]
    all_to_all x2, waiting for transfers between devices: 16.5 us -> 13.2 us  [fetch_blocks(): lax.all_to_all(replies, 'angle', split_axis=0, concat_axis=0, tiled=True)]
    ppermute x4 -> x6, starting transfers between devices: 12.1 us -> 8.95 us  [the longest x1 4.88 us: shards(): before = lax.ppermute(projection[:, :, band_rows - HALO:], 'tile', up)]
    all_to_all x1, waiting for transfers between devices: 1.51 us -> 3.78 us  [shards(): lax.all_to_all(requests, 'angle', split_axis=0, concat_axis=0, tiled=True)]
    ppermute x4 -> x6, waiting for transfers between devices: 3.58 us -> 1.54 us  [the longest x2 1.17 us: swap_half(): return lax.ppermute(value, 'half', [(0, 1), (1, 0)])]
  transfers between devices with their start and end apart: 8 -> 10, of which waited for: 5 -> 6; matrix products, arithmetic and copies ran while one was open for 6% -> 12% of each run, Pallas kernels for 0% -> 11%
where the time goes in v1:
time: 82.6 us; the launch traced here: 81.8 us
  starting transfers between devices  26.4 us (32%)
  waiting for transfers between devices  25.7 us (31%)
  local copies, waits for them, and re-layouts  12.3 us (15%)
  Pallas kernels  9.08 us (11%)
  other arithmetic  5.23 us (6%)
  matrix products  2.05 us (2%)
  between operations  1.02 us (1%)
    all_to_all x2, waiting for transfers between devices, fetch_blocks(): lax.all_to_all(replies, 'angle', split_axis=0, concat_axis=0, tiled=True)  13.2 us
    pallas_call x1, Pallas kernels, patch_sums(): pl.pallas_call(ptycho_kernel, out_shape=(rim, jax.ShapeDtypeStruct(own.sh...  9.08 us
    all_to_all x1, waiting for transfers between devices, shards(): lax.all_to_all(outgoing.reshape(groups, capacity, slice_rows, PIX).astype...  7.15 us
    all_to_all x1, starting transfers between devices, shards(): lax.all_to_all(requests, 'angle', split_axis=0, concat_axis=0, tiled=True)  6.98 us
    all_to_all x2, starting transfers between devices, fetch_blocks(): lax.all_to_all(replies, 'angle', split_axis=0, concat_axis=0, tiled=True)  6.97 us
    ppermute x1, starting transfers between devices, shards(): before = lax.ppermute(projection[:, :, band_rows - HALO:], 'tile', up)  4.88 us
    all_to_all x1, waiting for transfers between devices, shards(): lax.all_to_all(requests, 'angle', split_axis=0, concat_axis=0, tiled=True)  3.78 us
    all_to_all x1, starting transfers between devices, shards(): lax.all_to_all(outgoing.reshape(groups, capacity, slice_rows, PIX).astype...  3.53 us
  transfers between devices with their start and end apart: 10, of which 6 were waited for; matrix products, arithmetic and copies ran while one was open for 12% of the time, Pallas kernels for 11%

profile of v1, /device:TPU:0, one launch (start us, length us, event | category | flops | bytes accessed | tf_op | source)
XLA Modules:
  0.0 81.8 jit_solution(10138904509214179072)
XLA Ops:
  0.6 1.4 %collective-permute-start.1 = (f32[1,2,32,256]{3,2,1,0:T(8,128)}, f32[1,2,32,256]{3,2,1,0:T(8,128)S(1)}, u32[]{:S(2)}, u32[]{:S(2)}) collective-permute-start(f32[1,2,32,256]{3,2,1,0:T(8,128)} %own_ref.1), channel_id=1, source_target_pairs={{2,0},{3,1},{6,4},{7,5},{10,8},{11,9},{14,12},{15,13},{18,16},{19,... | collective-permute-start | bytes 196616 | tf_op jit(solution)/shard_map/ppermute | solution.py:195
  2.1 4.9 %collective-permute-start = (f32[1,2,32,256]{3,2,1,0:T(8,128)}, f32[1,2,32,256]{3,2,1,0:T(8,128)S(1)}, u32[]{:S(2)}, u32[]{:S(2)}) collective-permute-start(f32[1,2,32,256]{3,2,1,0:T(8,128)} %own_ref.1), channel_id=1, source_target_pairs={{0,2},{1,3},{4,6},{5,7},{8,10},{9,11},{12,14},{13,15},{16,18},{17,... | collective-permute-start | bytes 196616 | tf_op jit(solution)/shard_map/ppermute | solution.py:194
  7.0 0.8 reshape.188
  10.1 7.0 %all-to-all-start = ((s32[8,1,2]{2,1,0:T(1,128)}), s32[8,1,2]{2,1,0:T(1,128)S(1)}, u32[]{:S(2)}, u32[]{:S(2)}) async-start(s32[8,1,2]{2,1,0:T(1,128)} %bitcast.3), calls=%async_computation | async-start | bytes 8192 | tf_op jit(solution)/shard_map/all_to_all | solution.py:230
  17.1 0.8 slice_select_fusion.2
  18.7 1.1 %convert_element_type.36 = bf16[16,16,512]{2,1,0:T(8,128)(2,1)S(1)} convert(f32[16,16,512]{2,1,0:T(8,128)} %param.27) | non-fusion elementwise | flops 131072 | bytes 786432 | tf_op jit(solution)/shard_map/convert_element_type | solution.py:236
  19.7 3.8 %all-to-all-done = s32[8,1,2]{2,1,0:T(1,128)S(1)} async-done(((s32[8,1,2]{2,1,0:T(1,128)}), s32[8,1,2]{2,1,0:T(1,128)S(1)}, u32[]{:S(2)}, u32[]{:S(2)}) %all-to-all-start) | async-done | bytes 96 | tf_op jit(solution)/shard_map/all_to_all | solution.py:230
  24.9 9.1 %shard_map.175 = (f32[1,2,32,256]{3,2,1,0:T(8,128)}, f32[1,2,32,256]{3,2,1,0:T(8,128)}, f32[1,2,32,256]{3,2,1,0:T(8,128)}) custom-call(s32[1,32]{1,0:T(1,128)} %rows_ref.1, s32[1,32]{1,0:T(1,128)} %cols_ref.1, f32[1,2,32,256]{3,2,1,0:T(8,128)} %copy-done.11, f32[1,2,32,256]{3,2,1,0:T(8,128)} %own_ref.1, f32[1,2,32,256]{3,2,1,0:T(8,128)} %copy-done.10, ...), custom_call_target="tpu_custom_call" | custom-call | flops 2000000000 | bytes 2000000 | tf_op jit(solution)/shard_map/pallas_call | solution.py:147
  34.0 1.3 %collective-permute-start.2 = (f32[1,2,32,256]{3,2,1,0:T(8,128)}, f32[1,2,32,256]{3,2,1,0:T(8,128)S(1)}, u32[]{:S(2)}, u32[]{:S(2)}) collective-permute-start(f32[1,2,32,256]{3,2,1,0:T(8,128)} %get-tuple-element.7), channel_id=1, source_target_pairs={{0,2},{1,3},{4,6},{5,7},{8,10},{9,11},{12,14},{13,15},{16,18},{17,... | collective-permute-start | bytes 196616 | tf_op jit(solution)/shard_map/ppermute | solution.py:200
  35.3 1.3 %collective-permute-start.3 = (f32[1,2,32,256]{3,2,1,0:T(8,128)}, f32[1,2,32,256]{3,2,1,0:T(8,128)S(1)}, u32[]{:S(2)}, u32[]{:S(2)}) collective-permute-start(f32[1,2,32,256]{3,2,1,0:T(8,128)} %get-tuple-element.8), channel_id=1, source_target_pairs={{2,0},{3,1},{6,4},{7,5},{10,8},{11,9},{14,12},{15,13},{18,16},{19,... | collective-permute-start | bytes 196616 | tf_op jit(solution)/shard_map/ppermute | solution.py:201
  36.6 1.3 %gather_fusion = bf16[16,16,512]{2,1,0:T(8,128)(2,1)} fusion(bf16[16,16,512]{2,1,0:T(8,128)(2,1)S(1)} %convert_element_type.36, s32[1024]{0:T(1024)S(1)} %pad_clamp_fusion.1), kind=kCustom, calls=%fused_computation | custom fusion | bytes 524352 | tf_op jit(solution)/shard_map/gather | solution.py:236
  37.9 3.4 %all-to-all-start.1 = ((bf16[8,2,16,512]{3,2,1,0:T(8,128)(2,1)}), bf16[8,2,16,512]{3,2,1,0:T(8,128)(2,1)S(1)}, u32[]{:S(2)}, u32[]{:S(2)}) async-start(bf16[8,2,16,512]{3,2,1,0:T(8,128)(2,1)} %bitcast.6), calls=%async_computation.1 | async-start | bytes 524288 | tf_op jit(solution)/shard_map/all_to_all | solution.py:237
  41.7 0.9 %multiply_subtract_fusion = f32[1,2,32,256]{3,2,1,0:T(8,128)S(1)} fusion(f32[1,2,32,256]{3,2,1,0:T(8,128)S(1)} %copy-done.8, f32[1,2,32,256]{3,2,1,0:T(8,128)S(1)} %copy-done.2, f32[1,1,32,256]{3,2,1,0:T(8,128)S(1)} %bitcast.67, f32[1,2,32,256]{3,2,1,0:T(8,128)S(1)} %collective-permute-done.3, f32[1,2,32,256]{3,2,1,0:T(8,128)} %get-tuple-element.6, ...), kind=kLoop, calls=%fused_computation.27 | loop fusion | flops 131072 | bytes 425984 | tf_op jit(solution)/shard_map/sub | solution.py:208
  42.7 1.2 %collective-permute-done.4 = f32[1,2,16,256]{3,2,1,0:T(8,128)S(1)} collective-permute-done((f32[1,2,16,256]{3,2,1,0:T(8,128)S(1)}, f32[1,2,16,256]{3,2,1,0:T(8,128)S(1)}, u32[]{:S(2)}, u32[]{:S(2)}) %collective-permute-start.4) | collective-permute-done | bytes 32800 | tf_op jit(solution)/shard_map/ppermute | solution.py:164
  43.9 5.8 %all-to-all-done.1 = bf16[8,2,16,512]{3,2,1,0:T(8,128)(2,1)S(1)} async-done(((bf16[8,2,16,512]{3,2,1,0:T(8,128)(2,1)}), bf16[8,2,16,512]{3,2,1,0:T(8,128)(2,1)S(1)}, u32[]{:S(2)}, u32[]{:S(2)}) %all-to-all-start.1) | async-done | bytes 262176 | tf_op jit(solution)/shard_map/all_to_all | solution.py:237
  50.3 1.0 %convolution_multiply_fusion = f32[2,2,16,4,512]{4,2,3,1,0:T(8,128)S(1)} fusion(bf16[2,2,4,128,512]{4,3,2,1,0:T(8,128)(2,1)S(1)} %copy-done, f32[2,2,4]{2,1,0:T(2,128)S(1)} %get-tuple-element.23, bf16[2,2,4,16,512]{4,3,2,1,0:T(8,128)(2,1)S(1)} %bitcast.61, bf16[2,2,4]{2,1,0:T(2,128)(2,1)S(1)} %get-tuple-element.22, f32[2,16,2,128]{3,2,1,0:T(2,128)S(1)} %add.90), kind=kOutput, calls=%fused_computation.8 | convolution fusion | flops 67387392 | bytes 2916448 | tf_op jit(solution)/shard_map/tkcrp,tskr->tkcsp/dot_general | solution.py:248
  51.4 1.1 %scatter_fusion = f32[16,16,512]{2,1,0:T(8,128)S(1)} fusion(f32[16,16,512]{2,1,0:T(8,128)S(1)} %broadcast_in_dim.2, s32[16]{0:T(128)S(1)} %fusion.24, f32[16,16,512]{2,1,0:T(8,128)S(1)} %bitcast.60), kind=kCustom, calls=%fused_computation.5 | custom fusion | bytes 1572928 | tf_op jit(solution)/shard_map/scatter | solution.py:254
  52.5 1.0 %copy.33 = bf16[8,2,16,512]{3,1,2,0:T(2,128)(2,1)} copy(bf16[8,2,16,512]{3,2,1,0:T(8,128)(2,1)S(1)} %bitcast.63) | data formatting | bytes 524288 | tf_op jit(solution)/shard_map/convert_element_type | solution.py:257
  53.5 3.5 %all-to-all-start.2 = ((bf16[8,2,16,512]{3,1,2,0:T(2,128)(2,1)}), bf16[8,2,16,512]{3,1,2,0:T(2,128)(2,1)S(1)}, u32[]{:S(2)}, u32[]{:S(2)}) async-start(bf16[8,2,16,512]{3,1,2,0:T(2,128)(2,1)} %copy.33), calls=%async_computation.2 | async-start | bytes 524288 | tf_op jit(solution)/shard_map/all_to_all | solution.py:256
  58.4 7.1 %all-to-all-done.2 = bf16[8,2,16,512]{3,1,2,0:T(2,128)(2,1)S(1)} async-done(((bf16[8,2,16,512]{3,1,2,0:T(2,128)(2,1)}), bf16[8,2,16,512]{3,1,2,0:T(2,128)(2,1)S(1)}, u32[]{:S(2)}, u32[]{:S(2)}) %all-to-all-start.2) | async-done | bytes 262176 | tf_op jit(solution)/shard_map/all_to_all | solution.py:256
  66.5 1.3 %gather_fusion.2 = bf16[16,16,512]{2,1,0:T(8,128)(2,1)} fusion(bf16[16,16,512]{2,1,0:T(8,128)(2,1)S(1)} %copy.37, s32[1024]{0:T(1024)S(1)} %pad_clamp_fusion.1), kind=kCustom, calls=%fused_computation.2 | custom fusion | bytes 524352 | tf_op jit(solution)/shard_map/gather | solution.py:236
  67.7 3.6 %all-to-all-start.3 = ((bf16[8,2,16,512]{3,2,1,0:T(8,128)(2,1)}), bf16[8,2,16,512]{3,2,1,0:T(8,128)(2,1)S(1)}, u32[]{:S(2)}, u32[]{:S(2)}) async-start(bf16[8,2,16,512]{3,2,1,0:T(8,128)(2,1)} %bitcast.17), calls=%async_computation.3 | async-start | bytes 524288 | tf_op jit(solution)/shard_map/all_to_all | solution.py:237
  71.3 1.1 %copy.39 = f32[16,16,512]{2,1,0:T(8,128)} copy(f32[16,16,512]{2,0,1:T(8,128)S(1)} %get-tuple-element.27) | data formatting | bytes 1048576
  72.4 7.4 %all-to-all-done.3 = bf16[8,2,16,512]{3,2,1,0:T(8,128)(2,1)S(1)} async-done(((bf16[8,2,16,512]{3,2,1,0:T(8,128)(2,1)}), bf16[8,2,16,512]{3,2,1,0:T(8,128)(2,1)S(1)}, u32[]{:S(2)}, u32[]{:S(2)}) %all-to-all-start.3) | async-done | bytes 262176 | tf_op jit(solution)/shard_map/all_to_all | solution.py:237
  (64 shorter events, 9.9 us)
Async XLA Ops:
  0.6 49.7 %copy-start = (bf16[2,2,4,128,512]{4,3,2,1,0:T(8,128)(2,1)S(1)}, bf16[2,2,4,128,512]{4,3,2,1,0:T(8,128)(2,1)}, u32[]{:S(2)}) copy-start(bf16[2,2,4,128,512]{4,3,2,1,0:T(8,128)(2,1)} %param.24) | copy-start | bytes 6291460
  0.6 23.0 %collective-permute-start.1 = (f32[1,2,32,256]{3,2,1,0:T(8,128)}, f32[1,2,32,256]{3,2,1,0:T(8,128)S(1)}, u32[]{:S(2)}, u32[]{:S(2)}) collective-permute-start(f32[1,2,32,256]{3,2,1,0:T(8,128)} %own_ref.1), channel_id=1, source_target_pairs={{2,0},{3,1},{6,4},{7,5},{10,8},{11,9},{14,12},{15,13},{18,16},{19,... | collective-permute-start | bytes 196616 | tf_op jit(solution)/shard_map/ppermute | solution.py:195
  2.1 21.6 %collective-permute-start = (f32[1,2,32,256]{3,2,1,0:T(8,128)}, f32[1,2,32,256]{3,2,1,0:T(8,128)S(1)}, u32[]{:S(2)}, u32[]{:S(2)}) collective-permute-start(f32[1,2,32,256]{3,2,1,0:T(8,128)} %own_ref.1), channel_id=1, source_target_pairs={{0,2},{1,3},{4,6},{5,7},{8,10},{9,11},{12,14},{13,15},{16,18},{17,... | collective-permute-start | bytes 196616 | tf_op jit(solution)/shard_map/ppermute | solution.py:194
  10.1 13.4 %all-to-all-start = ((s32[8,1,2]{2,1,0:T(1,128)}), s32[8,1,2]{2,1,0:T(1,128)S(1)}, u32[]{:S(2)}, u32[]{:S(2)}) async-start(s32[8,1,2]{2,1,0:T(1,128)} %bitcast.3), calls=%async_computation | async-start | bytes 8192 | tf_op jit(solution)/shard_map/all_to_all | solution.py:230
  17.9 24.8 %collective-permute-start.5 = (f32[1,2,16,256]{3,2,1,0:T(8,128)S(1)}, f32[1,2,16,256]{3,2,1,0:T(8,128)S(1)}, u32[]{:S(2)}, u32[]{:S(2)}) collective-permute-start(f32[1,2,16,256]{3,2,1,0:T(8,128)S(1)} %slice_select_fusion.2), channel_id=1, source_target_pairs={{0,1},{1,0},{2,3},{3,2},{4,5},{5,4},{6,7},{7,6},{8,9},{9,8},{10,11... | collective-permute-start | bytes 98312 | tf_op jit(solution)/shard_map/ppermute | solution.py:164
  23.6 18.0 %copy-start.2 = (f32[1,2,32,256]{3,2,1,0:T(8,128)S(1)}, f32[1,2,32,256]{3,2,1,0:T(8,128)}, u32[]{:S(2)}) copy-start(f32[1,2,32,256]{3,2,1,0:T(8,128)} %param.17) | copy-start | bytes 196612
  23.6 18.0 %copy-start.8 = (f32[1,2,32,256]{3,2,1,0:T(8,128)S(1)}, f32[1,2,32,256]{3,2,1,0:T(8,128)}, u32[]{:S(2)}) copy-start(f32[1,2,32,256]{3,2,1,0:T(8,128)} %own_ref.1) | copy-start | bytes 196612
  23.6 18.0 %copy-start.9 = (f32[1,32,256]{2,1,0:T(8,128)S(1)}, f32[1,32,256]{2,1,0:T(8,128)}, u32[]{:S(2)}) copy-start(f32[1,32,256]{2,1,0:T(8,128)} %param.18) | copy-start | bytes 98308
  23.7 0.6 copy-start.10
  24.3 0.6 copy-start.11
  34.0 7.3 %collective-permute-start.2 = (f32[1,2,32,256]{3,2,1,0:T(8,128)}, f32[1,2,32,256]{3,2,1,0:T(8,128)S(1)}, u32[]{:S(2)}, u32[]{:S(2)}) collective-permute-start(f32[1,2,32,256]{3,2,1,0:T(8,128)} %get-tuple-element.7), channel_id=1, source_target_pairs={{0,2},{1,3},{4,6},{5,7},{8,10},{9,11},{12,14},{13,15},{16,18},{17,... | collective-permute-start | bytes 196616 | tf_op jit(solution)/shard_map/ppermute | solution.py:200
  35.3 6.4 %collective-permute-start.3 = (f32[1,2,32,256]{3,2,1,0:T(8,128)}, f32[1,2,32,256]{3,2,1,0:T(8,128)S(1)}, u32[]{:S(2)}, u32[]{:S(2)}) collective-permute-start(f32[1,2,32,256]{3,2,1,0:T(8,128)} %get-tuple-element.8), channel_id=1, source_target_pairs={{2,0},{3,1},{6,4},{7,5},{10,8},{11,9},{14,12},{15,13},{18,16},{19,... | collective-permute-start | bytes 196616 | tf_op jit(solution)/shard_map/ppermute | solution.py:201
  37.9 11.9 %all-to-all-start.1 = ((bf16[8,2,16,512]{3,2,1,0:T(8,128)(2,1)}), bf16[8,2,16,512]{3,2,1,0:T(8,128)(2,1)S(1)}, u32[]{:S(2)}, u32[]{:S(2)}) async-start(bf16[8,2,16,512]{3,2,1,0:T(8,128)(2,1)} %bitcast.6), calls=%async_computation.1 | async-start | bytes 524288 | tf_op jit(solution)/shard_map/all_to_all | solution.py:237
  42.5 8.7 %copy-start.3 = (f32[1,2,32,256]{3,2,1,0:T(8,128)}, f32[1,2,32,256]{3,2,1,0:T(8,128)S(1)}, u32[]{:S(2)}) copy-start(f32[1,2,32,256]{3,2,1,0:T(8,128)S(1)} %multiply_subtract_fusion) | copy-start | bytes 196612
  42.6 1.3 %collective-permute-start.4 = (f32[1,2,16,256]{3,2,1,0:T(8,128)S(1)}, f32[1,2,16,256]{3,2,1,0:T(8,128)S(1)}, u32[]{:S(2)}, u32[]{:S(2)}) collective-permute-start(f32[1,2,16,256]{3,2,1,0:T(8,128)S(1)} %slice_select_fusion), channel_id=1, source_target_pairs={{0,1},{1,0},{2,3},{3,2},{4,5},{5,4},{6,7},{7,6},{8,9},{9,8},{10,11... | collective-permute-start | bytes 98312 | tf_op jit(solution)/shard_map/ppermute | solution.py:164
  43.9 5.9 %copy-start.4 = (f32[1,2,16,256]{3,2,1,0:T(8,128)}, f32[1,2,16,256]{3,2,1,0:T(8,128)S(1)}, u32[]{:S(2)}) copy-start(f32[1,2,16,256]{3,2,1,0:T(8,128)S(1)} %get-tuple-element.18) | copy-start | bytes 98308
  43.9 5.9 %copy-start.6 = (f32[1,2,16,256]{3,2,1,0:T(8,128)}, f32[1,2,16,256]{3,2,1,0:T(8,128)S(1)}, u32[]{:S(2)}) copy-start(f32[1,2,16,256]{3,2,1,0:T(8,128)S(1)} %get-tuple-element.19) | copy-start | bytes 98308
  52.4 13.4 %copy-start.1 = (f32[16,16,512]{2,1,0:T(8,128)S(1)}, f32[16,16,512]{2,1,0:T(8,128)}, u32[]{:S(2)}) copy-start(f32[16,16,512]{2,1,0:T(8,128)} %param.27) | copy-start | bytes 1572868
  53.5 12.1 %all-to-all-start.2 = ((bf16[8,2,16,512]{3,1,2,0:T(2,128)(2,1)}), bf16[8,2,16,512]{3,1,2,0:T(2,128)(2,1)S(1)}, u32[]{:S(2)}, u32[]{:S(2)}) async-start(bf16[8,2,16,512]{3,1,2,0:T(2,128)(2,1)} %copy.33), calls=%async_computation.2 | async-start | bytes 524288 | tf_op jit(solution)/shard_map/all_to_all | solution.py:256
  67.7 12.1 %all-to-all-start.3 = ((bf16[8,2,16,512]{3,2,1,0:T(8,128)(2,1)}), bf16[8,2,16,512]{3,2,1,0:T(8,128)(2,1)S(1)}, u32[]{:S(2)}, u32[]{:S(2)}) async-start(bf16[8,2,16,512]{3,2,1,0:T(8,128)(2,1)} %bitcast.17), calls=%async_computation.3 | async-start | bytes 524288 | tf_op jit(solution)/shard_map/all_to_all | solution.py:237
  71.3 9.9 %copy-start.5 = (f32[1,2,16,256]{3,2,1,0:T(8,128)S(1)}, f32[1,2,16,256]{3,2,1,0:T(8,128)}, u32[]{:S(2)}) copy-start(f32[1,2,16,256]{3,2,1,0:T(8,128)} %copy-done.4) | copy-start | bytes 98308
  71.3 9.9 %copy-start.7 = (f32[1,2,16,256]{3,2,1,0:T(8,128)S(1)}, f32[1,2,16,256]{3,2,1,0:T(8,128)}, u32[]{:S(2)}) copy-start(f32[1,2,16,256]{3,2,1,0:T(8,128)} %copy-done.6) | copy-start | bytes 98308

commit v2 on v1

--- a/solution.py
+++ b/solution.py
@@ -1,3 +1,5 @@
+import functools
+
 import jax
 import jax.numpy as jnp
 import numpy as np
@@ -20,7 +22,6 @@
 descent = 0.25
 volume_step = 1.0
 damping = 0.1
-highest = lax.Precision.HIGHEST
 
 
 def neighbours(axis):
@@ -160,19 +161,244 @@
     )(rows, cols, before, own, after, measured, field, mask, *tables)
 
 
-def swap_half(value):
-    return lax.ppermute(value, "half", [(0, 1), (1, 0)])
-
-
-def to_slices(value):
-    side = lax.axis_index("half")
-    rows = value.shape[2] // 2
-    low, high = value[:, :, :rows], value[:, :, rows:]
-    kept = jnp.where(side == 0, low, high)
-    other = swap_half(jnp.where(side == 0, high, low))
-    return jnp.concatenate(
-        [jnp.where(side == 0, kept, other), jnp.where(side == 0, other, kept)], axis=0
-    )
+MESH = pl.DeviceIdType.MESH
+
+
+def tail_kernel(
+    groups, tiles, capacity,
+    wanted_ref, place_ref, slot_ref, used_ref, live_ref,
+    top_ref, mid_ref, bottom_ref, proj_ref, mult_ref, prior_ref, weight_ref, vol_ref,
+    updated_ref, new_vol_ref, new_mult_ref,
+    above_ref, below_ref, moved_ref, mult_moved_ref, half_send_ref,
+    send_a, send_b, send_c, recv_a, recv_b, recv_c, spread_ref, wide_ref,
+    send_sem, recv_sem, near_send, near_recv,
+):
+    g = lax.axis_index("angle")
+    t = lax.axis_index("tile")
+    h = lax.axis_index("half")
+    band = proj_ref.shape[2]
+    part = band // 2
+    places = groups * capacity
+    slots = weight_ref.shape[0]
+    own_blocks = vol_ref.shape[0]
+    has_up = t > 0
+    has_down = t < tiles - 1
+    half = jnp.bfloat16
+    sends = (send_a, send_b, send_c)
+    recvs = (recv_a, recv_b, recv_c)
+
+    barrier = pltpu.get_barrier_semaphore()
+
+    def greet(where):
+        pl.semaphore_signal(barrier, inc=1, device_id=where, device_id_type=MESH)
+
+    for d in range(1, groups):
+        greet({"angle": lax.rem(g + d, groups)})
+    greet({"half": 1 - h})
+
+    @pl.when(has_up)
+    def _():
+        greet({"tile": t - 1})
+
+    @pl.when(has_down)
+    def _():
+        greet({"tile": t + 1})
+
+    def pick(n, carry):
+        send_a[n] = vol_ref[wanted_ref[n]].astype(half)
+        return carry
+
+    lax.fori_loop(0, places, pick, 0, unroll=True)
+    pl.semaphore_wait(barrier, groups + has_up.astype(jnp.int32) + has_down.astype(jnp.int32))
+
+    def exchange(phase):
+        copies = []
+        for d in range(1, groups):
+            peer = lax.rem(g + d, groups)
+            copy = pltpu.make_async_remote_copy(
+                src_ref=sends[phase].at[pl.ds(peer * capacity, capacity)],
+                dst_ref=recvs[phase].at[pl.ds(g * capacity, capacity)],
+                send_sem=send_sem.at[phase, d],
+                recv_sem=recv_sem.at[phase, d],
+                device_id={"angle": peer},
+                device_id_type=MESH,
+            )
+            copy.start()
+            copies.append(copy)
+        own = pl.ds(g * capacity, capacity)
+        recvs[phase][own] = sends[phase][own]
+        return copies
+
+    def near(index, source, target, where):
+        return pltpu.make_async_remote_copy(
+            src_ref=source,
+            dst_ref=target,
+            send_sem=near_send.at[index],
+            recv_sem=near_recv.at[index],
+            device_id=where,
+            device_id_type=MESH,
+        )
+
+    down_copy = near(0, bottom_ref, above_ref, {"tile": jnp.minimum(t + 1, tiles - 1)})
+    up_copy = near(1, top_ref, below_ref, {"tile": jnp.maximum(t - 1, 0)})
+
+    @pl.when(has_down)
+    def _():
+        down_copy.start()
+
+    @pl.when(has_up)
+    def _():
+        up_copy.start()
+
+    away = pl.ds(pl.multiple_of((1 - h) * part, part), part)
+    here = pl.ds(pl.multiple_of(h * part, part), part)
+    mult_copy = near(2, mult_ref.at[0, :, away, :], mult_moved_ref.at[h], {"half": 1 - h})
+    mult_copy.start()
+    fetches = exchange(0)
+    mult_moved_ref[h] = mult_ref[0, :, here, :]
+
+    @pl.when(jnp.logical_not(has_up))
+    def _():
+        above_ref[...] = jnp.zeros_like(above_ref)
+
+    @pl.when(jnp.logical_not(has_down))
+    def _():
+        below_ref[...] = jnp.zeros_like(below_ref)
+
+    @pl.when(has_up)
+    def _():
+        down_copy.wait_recv()
+
+    @pl.when(has_down)
+    def _():
+        up_copy.wait_recv()
+
+    old = proj_ref[0]
+    base = mid_ref[0]
+    if band == HALO:
+        gradient = base + above_ref[0] + below_ref[0]
+    else:
+        still = jnp.zeros((2, band - HALO, NW), jnp.float32)
+        gradient = base + jnp.concatenate([above_ref[0], still], axis=1)
+        gradient = gradient + jnp.concatenate([still, below_ref[0]], axis=1)
+    new_re = old[0] - descent * (gradient[0] + penalty * (old[0] - 1.0) + mult_ref[0, 0])
+    new_im = old[1] - descent * (gradient[1] + penalty * (old[1] - prior_ref[0]) + mult_ref[0, 1])
+    updated_ref[0, 0] = new_re
+    updated_ref[0, 1] = new_im
+    half_send_ref[...] = updated_ref[0, :, away, :]
+    moved_copy = near(3, half_send_ref, moved_ref.at[h], {"half": 1 - h})
+    moved_copy.start()
+    moved_ref[h] = updated_ref[0, :, here, :]
+    for copy in fetches:
+        copy.wait_recv()
+    mult_copy.wait_recv()
+
+    per_block = CMAX
+
+    def projected(phase, pair):
+        total = jnp.zeros((part, RB), jnp.float32)
+        for c in range(per_block):
+            slot = pair * per_block + c
+            picked = recvs[phase][place_ref[slot]]
+            total = total + live_ref[slot] * lax.dot_general(
+                picked, weight_ref[slot], (((1,), (1,)), ((), ())),
+                preferred_element_type=jnp.float32,
+            )
+        return total
+
+    pairs = slots // per_block
+    sinos = [projected(0, pair) for pair in range(pairs)]
+    moved_copy.wait_recv()
+    for pair in range(pairs):
+        angle, k = divmod(pair, NRB)
+        rays = slice(k * RB, (k + 1) * RB)
+        target = moved_ref[angle, 1, :, rays] + mult_moved_ref[angle, 1, :, rays] / penalty
+        residual = (sinos[pair] - target).astype(half)
+        for c in range(per_block):
+            slot = pair * per_block + c
+            spread = live_ref[slot] * jnp.dot(
+                residual, weight_ref[slot], preferred_element_type=jnp.float32
+            )
+            spread_ref[slot] = spread.astype(half)
+    for n in range(places):
+        send_b[n] = spread_ref[slot_ref[n]] * used_ref[n].astype(half)
+    terms = exchange(1)
+    for copy in terms:
+        copy.wait_recv()
+    for n in range(places):
+        wide_ref[n] = recv_b[n].astype(jnp.float32)
+
+    def renew(j, carry):
+        total = jnp.zeros(wide_ref.shape[1:], jnp.float32)
+        for n in range(places):
+            total = total + jnp.where(wanted_ref[n] == j, 1.0, 0.0) * wide_ref[n]
+        block = vol_ref[j]
+        new_vol_ref[j] = block - volume_step * (total + damping * block)
+        return carry
+
+    lax.fori_loop(0, own_blocks, renew, 0)
+    for n in range(places):
+        send_c[n] = new_vol_ref[wanted_ref[n]].astype(half)
+    renewals = exchange(2)
+    for angle in range(moved_ref.shape[0]):
+        new_mult_ref[angle, 0] = mult_moved_ref[angle, 0] + penalty * (moved_ref[angle, 0] - 1.0)
+    for copy in renewals:
+        copy.wait_recv()
+    for pair in range(pairs):
+        angle, k = divmod(pair, NRB)
+        rays = slice(k * RB, (k + 1) * RB)
+        fresh = projected(2, pair)
+        new_mult_ref[angle, 1, :, rays] = mult_moved_ref[angle, 1, :, rays] + penalty * (
+            moved_ref[angle, 1, :, rays] - fresh
+        )
+    for copy in fetches + terms + renewals + [mult_copy, moved_copy]:
+        copy.wait_send()
+
+    @pl.when(has_down)
+    def _():
+        down_copy.wait_send()
+
+    @pl.when(has_up)
+    def _():
+        up_copy.wait_send()
+
+
+def finish(scalars, arrays, capacity):
+    top, mid, bottom, projection, multiplier, prior, weights, volume = arrays
+    groups = lax.axis_size("angle")
+    tiles = lax.axis_size("tile")
+    places = groups * capacity
+    slots = weights.shape[0]
+    part = projection.shape[2] // 2
+    vmem = pl.BlockSpec(memory_space=pltpu.VMEM)
+    smem = pl.BlockSpec(memory_space=pltpu.SMEM)
+    block = volume.shape[1:]
+    moved_shape = (2, 2, part, NW)
+    return pl.pallas_call(
+        functools.partial(tail_kernel, groups, tiles, capacity),
+        out_shape=(
+            jax.ShapeDtypeStruct(projection.shape, jnp.float32),
+            jax.ShapeDtypeStruct(volume.shape, jnp.float32),
+            jax.ShapeDtypeStruct(moved_shape, jnp.float32),
+        ),
+        in_specs=[smem] * 5 + [vmem] * 8,
+        out_specs=(vmem, vmem, vmem),
+        scratch_shapes=[
+            pltpu.VMEM(bottom.shape, jnp.float32),
+            pltpu.VMEM(top.shape, jnp.float32),
+            pltpu.VMEM(moved_shape, jnp.float32),
+            pltpu.VMEM(moved_shape, jnp.float32),
+            pltpu.VMEM(moved_shape[1:], jnp.float32),
+            *[pltpu.VMEM((places,) + block, jnp.bfloat16)] * 6,
+            pltpu.VMEM((slots,) + block, jnp.bfloat16),
+            pltpu.VMEM((places,) + block, jnp.float32),
+            pltpu.SemaphoreType.DMA((3, groups)),
+            pltpu.SemaphoreType.DMA((3, groups)),
+            pltpu.SemaphoreType.DMA((4,)),
+            pltpu.SemaphoreType.DMA((4,)),
+        ],
+        compiler_params=pltpu.CompilerParams(collective_id=1, has_side_effects=True),
+    )(*scalars, *arrays)
 
 
 def shards(
@@ -193,23 +419,10 @@
     band_rows = projection.shape[2]
     before = lax.ppermute(projection[:, :, band_rows - HALO :], "tile", up)
     after = lax.ppermute(projection[:, :, :HALO], "tile", down)
-    moved_mult = to_slices(multiplier)
     top, gradient, bottom = patch_sums(
         before, projection, after, row_start, column_start, intensity, probe_field, probe_mask
     )
-    from_above = lax.ppermute(bottom, "tile", up)
-    from_below = lax.ppermute(top, "tile", down)
-    if band_rows == HALO:
-        gradient = gradient + from_above + from_below
-    else:
-        gradient = gradient.at[:, :, :HALO].add(from_above)
-        gradient = gradient.at[:, :, band_rows - HALO :].add(from_below)
-    holder = jnp.stack([jnp.ones_like(reprojection), reprojection], axis=1)
-    updated = projection - descent * (gradient + penalty * (projection - holder) + multiplier)
-    moved = jnp.concatenate([to_slices(updated), moved_mult], axis=1)
-    target = moved[:, 1] + moved[:, 3] / penalty
     angle_count = weights.shape[0]
-    slice_rows = volume.shape[1]
     own_blocks = volume.shape[0]
     live = lax.iota(jnp.int32, CMAX)[None, None, :] < ray_counts[:, :, None]
     groups = lax.axis_size("angle")
@@ -230,48 +443,15 @@
     wanted = lax.all_to_all(requests, "angle", split_axis=0, concat_axis=0, tiled=True).reshape(
         groups * capacity
     )
-    live_half = live.astype(jnp.bfloat16)[:, :, :, None, None]
-
-    def fetch_blocks(field):
-        replies = field.astype(jnp.bfloat16)[wanted].reshape(groups, capacity, slice_rows, PIX)
-        arrived = lax.all_to_all(replies, "angle", split_axis=0, concat_axis=0, tiled=True)
-        picked = arrived.reshape(groups * capacity, slice_rows, PIX)[slot_place]
-        picked = picked.reshape(angle_count, NRB, CMAX, slice_rows, PIX) * live_half
-        result = jnp.einsum(
-            "tkcrp,tkcsp->tskr", weights, picked, preferred_element_type=jnp.float32
-        )
-        return result.reshape(angle_count, slice_rows, NW)
-
-    sinogram = fetch_blocks(volume)
-    residual = (sinogram - target).astype(jnp.bfloat16).reshape(angle_count, slice_rows, NRB, RB)
-    spread = (
-        jnp.einsum("tkcrp,tskr->tkcsp", weights, residual, preferred_element_type=jnp.float32)
-        * live.astype(jnp.float32)[:, :, :, None, None]
-    )
-    outgoing = (
-        jnp.zeros((groups * capacity, slice_rows, PIX), jnp.float32)
-        .at[slot_place]
-        .set(spread.reshape(slot_count, slice_rows, PIX))
-    )
-    incoming = lax.all_to_all(
-        outgoing.reshape(groups, capacity, slice_rows, PIX).astype(jnp.bfloat16),
-        "angle",
-        split_axis=0,
-        concat_axis=0,
-        tiled=True,
-    ).astype(jnp.float32)
-    placing = (wanted[:, None] == lax.iota(jnp.int32, own_blocks)[None, :]).astype(jnp.float32)
-    block_grad = jnp.einsum(
-        "nj,nsp->jsp",
-        placing,
-        incoming.reshape(groups * capacity, slice_rows, PIX),
-        precision=highest,
-    )
-    new_volume = volume - volume_step * (block_grad + damping * volume)
-    fresh = fetch_blocks(new_volume)
-    fresh_holder = jnp.stack([jnp.ones_like(fresh), fresh], axis=1)
-    new_multiplier = moved[:, 2:] + penalty * (moved[:, :2] - fresh_holder)
-    return (updated, new_volume, new_multiplier)
+    places = lax.iota(jnp.int32, groups * capacity)
+    hits = (places[:, None] == slot_place[None, :]).astype(jnp.int32)
+    place_slot = jnp.sum(hits * lax.iota(jnp.int32, slot_count)[None, :], axis=1)
+    place_used = jnp.sum(hits, axis=1).astype(jnp.float32)
+    live_scale = live.reshape(slot_count).astype(jnp.float32)
+    scalars = (wanted, slot_place, place_slot, place_used, live_scale)
+    tiles = weights.reshape(slot_count, RB, PIX)
+    arrays = (top, gradient, bottom, projection, multiplier, reprojection, tiles, volume)
+    return finish(scalars, arrays, capacity)
 
 
 def solution(mesh):

time: 82.6 us -> 66.2 us (0.80)
  Pallas kernels: 9.08 us -> 34.4 us
  waiting for transfers between devices: 25.7 us -> 3.81 us
  starting transfers between devices: 26.4 us -> 13.2 us
  other arithmetic: 5.23 us -> 2.96 us
  matrix products: 2.05 us -> 0 us
  local copies, waits for them, and re-layouts: 12.3 us -> 10.7 us
    pallas_call x0 -> x1, Pallas kernels: none -> 25.3 us  [finish(): pl.pallas_call(functools.partial(tail_kernel, groups, tiles, capacity), o...]
    all_to_all x3 -> x0, waiting for transfers between devices: 20.4 us -> none  [the longest x2 13.2 us: fetch_blocks(): lax.all_to_all(replies, 'angle', split_axis=0, concat_axis=0, tiled=True)]
    all_to_all x3 -> x0, starting transfers between devices: 10.5 us -> none  [the longest x2 6.97 us: fetch_blocks(): lax.all_to_all(replies, 'angle', split_axis=0, concat_axis=0, tiled=True)]
    unnamed x25 -> x9, local copies, waits for them, and re-layouts: 2.4 us -> 6.08 us
    gather x4 -> x0, local copies, waits for them, and re-layouts: 3.64 us -> none  [the longest x2 2.52 us: fetch_blocks(): field.astype(jnp.bfloat16)[wanted]]
    ppermute x4 -> x0, starting transfers between devices: 2.65 us -> none  [the longest x1 1.29 us: shards(): from_below = lax.ppermute(top, 'tile', down)]
    dot_general x3 -> x0, matrix products: 2.05 us -> none  [the longest x1 0.97 us: shards(): jnp.einsum('tkcrp,tskr->tkcsp', weights, residual, preferred_element_type...]
    ppermute x4 -> x0, waiting for transfers between devices: 1.53 us -> none  [the longest x2 1.17 us: swap_half(): return lax.ppermute(value, 'half', [(0, 1), (1, 0)])]
  transfers between devices with their start and end apart: 10 -> 3, of which waited for: 6 -> 1; matrix products, arithmetic and copies ran while one was open for 12% -> 10% of each run, Pallas kernels for 11% -> 0%
where the time goes in v2:
time: 66.2 us; the launch traced here: 65.7 us
  Pallas kernels  34.4 us (52%)
  starting transfers between devices  13.2 us (20%)
  local copies, waits for them, and re-layouts  10.7 us (16%)
  waiting for transfers between devices  3.81 us (6%)
  other arithmetic  2.96 us (4%)
  between operations  0.7 us (1%)
    pallas_call x1, Pallas kernels, finish(): pl.pallas_call(functools.partial(tail_kernel, groups, tiles, capacity), o...  25.3 us
    pallas_call x1, Pallas kernels, patch_sums(): pl.pallas_call(ptycho_kernel, out_shape=(rim, jax.ShapeDtypeStruct(own.sh...  9.07 us
    all_to_all x1, starting transfers between devices, shards(): lax.all_to_all(requests, 'angle', split_axis=0, concat_axis=0, tiled=True)  6.98 us
    unnamed x9, local copies, waits for them, and re-layouts  6.08 us
    ppermute x1, starting transfers between devices, shards(): before = lax.ppermute(projection[:, :, band_rows - HALO:], 'tile', up)  4.88 us
    all_to_all x1, waiting for transfers between devices, shards(): lax.all_to_all(requests, 'angle', split_axis=0, concat_axis=0, tiled=True)  3.8 us
    reshape x2, local copies, waits for them, and re-layouts, shards(): flat_ids = ray_blocks.reshape(slot_count)  1.53 us
  transfers between devices with their start and end apart: 3, of which 1 were waited for; matrix products, arithmetic and copies ran while one was open for 10% of the time, Pallas kernels for 0%

profile of v2, /device:TPU:0, one launch (start us, length us, event | category | flops | bytes accessed | tf_op | source)
XLA Modules:
  0.0 65.7 jit_solution(15977243912973502332)
XLA Ops:
  0.6 1.3 %collective-permute-start.1 = (f32[1,2,32,256]{3,2,1,0:T(8,128)}, f32[1,2,32,256]{3,2,1,0:T(8,128)S(1)}, u32[]{:S(2)}, u32[]{:S(2)}) collective-permute-start(f32[1,2,32,256]{3,2,1,0:T(8,128)} %proj_ref.1), channel_id=1, source_target_pairs={{2,0},{3,1},{6,4},{7,5},{10,8},{11,9},{14,12},{15,13},{18,16},{19,... | collective-permute-start | bytes 196616 | tf_op jit(solution)/shard_map/ppermute | solution.py:421
  1.9 4.9 %collective-permute-start = (f32[1,2,32,256]{3,2,1,0:T(8,128)}, f32[1,2,32,256]{3,2,1,0:T(8,128)S(1)}, u32[]{:S(2)}, u32[]{:S(2)}) collective-permute-start(f32[1,2,32,256]{3,2,1,0:T(8,128)} %proj_ref.1), channel_id=1, source_target_pairs={{0,2},{1,3},{4,6},{5,7},{8,10},{9,11},{12,14},{13,15},{16,18},{17,... | collective-permute-start | bytes 196616 | tf_op jit(solution)/shard_map/ppermute | solution.py:420
  6.8 0.8 %reshape.160 = s32[16]{0:T(128)S(1)} reshape(s32[2,2,4]{2,1,0:T(2,128)} %param.25) | data formatting | bytes 128 | tf_op jit(solution)/shard_map/reshape | solution.py:431
  7.6 0.8 %reshape.159 = s32[16,1]{0,1:T(1,128)S(1)} reshape(s32[2,2,4]{2,1,0:T(2,128)} %param.25) | data formatting | bytes 128 | tf_op jit(solution)/shard_map/reshape | solution.py:431
  8.4 0.1 fusion
  8.5 0.2 select_reduce_fusion.1
  8.7 0.6 scatter_custom_fusion
  9.3 0.7 %all_to_all.6 = s32[8,1,2]{2,0,1:T(8,128)} reshape(s32[16]{0:T(128)S(1)} %scatter_custom_fusion) | data formatting | bytes 128 | tf_op jit(solution)/shard_map/all_to_all | solution.py:443
  10.0 7.0 %all-to-all-start = ((s32[8,1,2]{2,1,0:T(1,128)}), s32[8,1,2]{2,1,0:T(1,128)S(1)}, u32[]{:S(2)}, u32[]{:S(2)}) async-start(s32[8,1,2]{2,1,0:T(1,128)} %bitcast.2), calls=%async_computation | async-start | bytes 8192 | tf_op jit(solution)/shard_map/all_to_all | solution.py:443
  17.0 0.8 %compare_convert_fusion = f32[2,2,4]{2,1,0:T(2,128)S(1)} fusion(s32[2,2]{1,0:T(2,128)} %param.26), kind=kLoop, calls=%fused_computation.7 | loop fusion | flops 32 | bytes 80 | tf_op jit(solution)/shard_map/convert_element_type | solution.py:450
  17.7 0.6 reshape.163.live_ref
  18.3 0.6 convert_reduce_fusion
  19.0 0.6 convert_element_type.16.used_ref
  19.6 3.8 %all-to-all-done = s32[8,1,2]{2,1,0:T(1,128)S(1)} async-done(((s32[8,1,2]{2,1,0:T(1,128)}), s32[8,1,2]{2,1,0:T(1,128)S(1)}, u32[]{:S(2)}, u32[]{:S(2)}) %all-to-all-start) | async-done | bytes 96 | tf_op jit(solution)/shard_map/all_to_all | solution.py:443
  23.4 0.5 broadcast.186
  23.9 0.7 %reduce.3 = s32[8,2]{1,0:T(8,128)S(1)} reduce(s32[8,1,2]{2,1,0:T(1,128)S(1)} %all-to-all-done, s32[]{:T(128)} %broadcast.186), dimensions={1}, to_apply=%all_to_all.7.reduce_sub_computation.3 | reduce | bytes 132 | tf_op jit(solution)/shard_map/all_to_all | solution.py:443
  24.6 0.7 reshape.161.wanted_ref
  25.2 0.6 copy-done.1
  25.8 0.6 copy-done.2
  26.5 9.1 %shard_map.175 = (f32[1,2,32,256]{3,2,1,0:T(8,128)}, f32[1,2,32,256]{3,2,1,0:T(8,128)}, f32[1,2,32,256]{3,2,1,0:T(8,128)}) custom-call(s32[1,32]{1,0:T(1,128)} %rows_ref.1, s32[1,32]{1,0:T(1,128)} %cols_ref.1, f32[1,2,32,256]{3,2,1,0:T(8,128)} %copy-done.2, f32[1,2,32,256]{3,2,1,0:T(8,128)} %proj_ref.1, f32[1,2,32,256]{3,2,1,0:T(8,128)} %copy-done.1, ...), custom_call_target="tpu_custom_call" | custom-call | flops 2000000000 | bytes 2000000 | tf_op jit(solution)/shard_map/pallas_call | solution.py:148
  35.5 25.3 %shard_map.176 = (f32[1,2,32,256]{3,2,1,0:T(8,128)}, f32[16,16,512]{2,1,0:T(8,128)}, f32[2,2,16,256]{3,2,1,0:T(8,128)}) custom-call(s32[16]{0:T(128)} %reshape.161.wanted_ref, s32[16]{0:T(128)} %copy-done, s32[16]{0:T(128)} %get-tuple-element.10.slot_ref, f32[16]{0:T(128)} %convert_element_type.16.used_ref, f32[16]{0:T(128)} %reshape.163.live_ref, ...), custom_call_target="tpu_custom_call" | custom-call | tf_op jit(solution)/shard_map/pallas_call | solution.py:377
  60.9 1.5 %copy.24 = f32[1,2,32,256]{3,2,1,0:T(8,128)} copy(f32[1,2,32,256]{3,2,1,0:T(8,128)} %get-tuple-element.16) | data formatting | bytes 131072
  62.3 1.9 %copy.25 = f32[16,16,512]{2,1,0:T(8,128)} copy(f32[16,16,512]{2,1,0:T(8,128)} %get-tuple-element.17) | data formatting | bytes 1048576
  64.2 1.5 %copy.26 = f32[2,2,16,256]{3,2,1,0:T(8,128)} copy(f32[2,2,16,256]{3,2,1,0:T(8,128)} %get-tuple-element.18) | data formatting | bytes 131072
  (10 shorter events, 0.1 us)
Async XLA Ops:
  0.6 24.6 %collective-permute-start.1 = (f32[1,2,32,256]{3,2,1,0:T(8,128)}, f32[1,2,32,256]{3,2,1,0:T(8,128)S(1)}, u32[]{:S(2)}, u32[]{:S(2)}) collective-permute-start(f32[1,2,32,256]{3,2,1,0:T(8,128)} %proj_ref.1), channel_id=1, source_target_pairs={{2,0},{3,1},{6,4},{7,5},{10,8},{11,9},{14,12},{15,13},{18,16},{19,... | collective-permute-start | bytes 196616 | tf_op jit(solution)/shard_map/ppermute | solution.py:421
  1.9 23.3 %collective-permute-start = (f32[1,2,32,256]{3,2,1,0:T(8,128)}, f32[1,2,32,256]{3,2,1,0:T(8,128)S(1)}, u32[]{:S(2)}, u32[]{:S(2)}) collective-permute-start(f32[1,2,32,256]{3,2,1,0:T(8,128)} %proj_ref.1), channel_id=1, source_target_pairs={{0,2},{1,3},{4,6},{5,7},{8,10},{9,11},{12,14},{13,15},{16,18},{17,... | collective-permute-start | bytes 196616 | tf_op jit(solution)/shard_map/ppermute | solution.py:420
  10.0 13.4 %all-to-all-start = ((s32[8,1,2]{2,1,0:T(1,128)}), s32[8,1,2]{2,1,0:T(1,128)S(1)}, u32[]{:S(2)}, u32[]{:S(2)}) async-start(s32[8,1,2]{2,1,0:T(1,128)} %bitcast.2), calls=%async_computation | async-start | bytes 8192 | tf_op jit(solution)/shard_map/all_to_all | solution.py:443
  17.0 18.6 %copy-start = (s32[16]{0:T(128)}, s32[16]{0:T(128)S(1)}, u32[]{:S(2)}) copy-start(s32[16]{0:T(128)S(1)} %multiply_add_fusion.place_ref) | copy-start | bytes 196
  25.2 0.6 copy-start.1
  25.8 0.6 copy-start.2

commit v3 on v2

--- a/solution.py
+++ b/solution.py
@@ -24,12 +24,6 @@
 damping = 0.1
 
 
-def neighbours(axis):
-    devices = lax.axis_size(axis)
-    up = [(i, i + 1) for i in range(devices - 1)]
-    return up, [(j, i) for i, j in up]
-
-
 def dft_blocks(sign):
     def table(length):
         counter = np.arange(length)
@@ -43,14 +37,188 @@
     return left.astype(np.float32), right.astype(np.float32)
 
 
+MESH = pl.DeviceIdType.MESH
+
+
+def head_kernel(groups, tiles, proj_ref, ids_ref, before_ref, after_ref, all_ref, near_send, near_recv, send_sem, recv_sem):
+    g = lax.axis_index("angle")
+    t = lax.axis_index("tile")
+    band = proj_ref.shape[2]
+    has_up = t > 0
+    has_down = t < tiles - 1
+    barrier = pltpu.get_barrier_semaphore()
+
+    def greet(where):
+        pl.semaphore_signal(barrier, inc=1, device_id=where, device_id_type=MESH)
+
+    for d in range(1, groups):
+        greet({"angle": lax.rem(g + d, groups)})
+
+    @pl.when(has_up)
+    def _():
+        greet({"tile": t - 1})
+
+    @pl.when(has_down)
+    def _():
+        greet({"tile": t + 1})
+
+    pl.semaphore_wait(barrier, groups - 1 + has_up.astype(jnp.int32) + has_down.astype(jnp.int32))
+    copies = []
+    for d in range(1, groups):
+        copy = pltpu.make_async_remote_copy(
+            src_ref=ids_ref,
+            dst_ref=all_ref.at[g],
+            send_sem=send_sem.at[d],
+            recv_sem=recv_sem.at[d],
+            device_id={"angle": lax.rem(g + d, groups)},
+            device_id_type=MESH,
+        )
+        copy.start()
+        copies.append(copy)
+
+    def near(index, source, target, where):
+        return pltpu.make_async_remote_copy(
+            src_ref=source,
+            dst_ref=target,
+            send_sem=near_send.at[index],
+            recv_sem=near_recv.at[index],
+            device_id=where,
+            device_id_type=MESH,
+        )
+
+    last = proj_ref.at[:, :, band - HALO :, :]
+    first = proj_ref.at[:, :, :HALO, :]
+    down_copy = near(0, last, before_ref, {"tile": jnp.minimum(t + 1, tiles - 1)})
+    up_copy = near(1, first, after_ref, {"tile": jnp.maximum(t - 1, 0)})
+
+    @pl.when(has_down)
+    def _():
+        down_copy.start()
+
+    @pl.when(has_up)
+    def _():
+        up_copy.start()
+
+    all_ref[g] = ids_ref[...]
+
+    @pl.when(jnp.logical_not(has_up))
+    def _():
+        before_ref[...] = jnp.zeros_like(before_ref)
+
+    @pl.when(jnp.logical_not(has_down))
+    def _():
+        after_ref[...] = jnp.zeros_like(after_ref)
+
+    @pl.when(has_up)
+    def _():
+        down_copy.wait_recv()
+        up_copy.wait_send()
+
+    @pl.when(has_down)
+    def _():
+        up_copy.wait_recv()
+        down_copy.wait_send()
+
+    for copy in copies:
+        copy.wait()
+
+
+def gather_head(projection, ray_blocks):
+    groups = lax.axis_size("angle")
+    tiles = lax.axis_size("tile")
+    slots = ray_blocks.size
+    vmem = pl.BlockSpec(memory_space=pltpu.VMEM)
+    rim = jax.ShapeDtypeStruct(projection.shape[:2] + (HALO, NW), jnp.float32)
+    return pl.pallas_call(
+        functools.partial(head_kernel, groups, tiles),
+        out_shape=(rim, rim, jax.ShapeDtypeStruct((groups, 1, slots), jnp.int32)),
+        in_specs=[vmem] * 2,
+        out_specs=(vmem, vmem, vmem),
+        scratch_shapes=[
+            pltpu.SemaphoreType.DMA((2,)),
+            pltpu.SemaphoreType.DMA((2,)),
+            pltpu.SemaphoreType.DMA((groups,)),
+            pltpu.SemaphoreType.DMA((groups,)),
+        ],
+        compiler_params=pltpu.CompilerParams(collective_id=2, has_side_effects=True),
+    )(projection, ray_blocks.reshape(1, slots))
+
+
+def fill_tables(own_blocks, all_ref, counts_ref, wanted_ref, place_ref, slot_ref, used_ref, live_ref):
+    g = lax.axis_index("angle")
+    groups, _, slots = all_ref.shape
+    capacity = wanted_ref.shape[0] // groups
+    mine = [all_ref[g, 0, s] for s in range(slots)]
+    owners = [lax.div(b, own_blocks) for b in mine]
+    for s in range(slots):
+        rank = jnp.int32(0)
+        for earlier in range(s):
+            rank = rank + jnp.where(owners[earlier] == owners[s], 1, 0)
+        place_ref[s] = owners[s] * capacity + rank
+        angle, block = divmod(s // CMAX, NRB)
+        live_ref[s] = jnp.where(s % CMAX < counts_ref[angle, block], 1.0, 0.0)
+
+    def clear(n, carry):
+        wanted_ref[n] = 0
+        slot_ref[n] = 0
+        used_ref[n] = 0.0
+        return carry
+
+    lax.fori_loop(0, groups * capacity, clear, 0)
+    for s in range(slots):
+        place = place_ref[s]
+        slot_ref[place] = s
+        used_ref[place] = 1.0
+
+    def group(peer, carry):
+        found = jnp.int32(0)
+        for s in range(slots):
+            b = all_ref[peer, 0, s]
+            hit = lax.div(b, own_blocks) == g
+
+            @pl.when(hit)
+            def _(found=found, b=b):
+                wanted_ref[peer * capacity + found] = lax.rem(b, own_blocks)
+
+            found = found + jnp.where(hit, 1, 0)
+        return carry
+
+    lax.fori_loop(0, groups, group, 0)
+
+
+def write_kernel(a_ref, b_ref, c_ref, a_out, b_out, c_out, sems):
+    copies = [
+        pltpu.make_async_copy(source, target, sems.at[i])
+        for i, (source, target) in enumerate(((a_ref, a_out), (b_ref, b_out), (c_ref, c_out)))
+    ]
+    for copy in copies:
+        copy.start()
+    for copy in copies:
+        copy.wait()
+
+
+def write_out(values):
+    return pl.pallas_call(
+        write_kernel,
+        out_shape=tuple(jax.ShapeDtypeStruct(v.shape, v.dtype) for v in values),
+        in_specs=[pl.BlockSpec(memory_space=pltpu.VMEM)] * 3,
+        out_specs=tuple([pl.BlockSpec(memory_space=pl.ANY)] * 3),
+        scratch_shapes=[pltpu.SemaphoreType.DMA((3,))],
+    )(*values)
+
+
 CHUNK = 4
 
 
 def ptycho_kernel(
-    rows_ref, cols_ref, before_ref, own_ref, after_ref, measured_ref, field_ref, mask_ref,
+    own_blocks, all_ref, counts_ref, rows_ref, cols_ref, before_ref, own_ref, after_ref, measured_ref, field_ref, mask_ref,
     left_f_ref, right_f_ref, left_b_ref, right_b_ref,
-    top_ref, mid_ref, bottom_ref, ext_ref, acc_ref, wave_ref,
+    top_ref, mid_ref, bottom_ref, wanted_ref, place_ref, slot_ref, used_ref, live_ref,
+    ext_ref, acc_ref, wave_ref,
 ):
+    fill_tables(
+        own_blocks, all_ref, counts_ref, wanted_ref, place_ref, slot_ref, used_ref, live_ref
+    )
     band = own_ref.shape[2]
     lanes = [slice(0, PC), slice(PC, NW)]
     for side in range(2):
@@ -136,8 +304,10 @@
         bottom_ref[0, :, :, lanes[side]] = acc_ref[:, side, HALO + band :]
 
 
-def patch_sums(before, own, after, rows, cols, measured, field, mask):
+def patch_sums(own_blocks, capacity, ids, counts, before, own, after, rows, cols, measured, field, mask):
     band = own.shape[2]
+    slots = ids.shape[2]
+    places = ids.shape[0] * capacity
     left_f, right_f = dft_blocks(-1.0)
     left_b, right_b = dft_blocks(1.0)
     tables = [jnp.asarray(m, jnp.bfloat16) for m in (left_f, right_f, left_b, right_b)]
@@ -146,10 +316,17 @@
     rim = jax.ShapeDtypeStruct(before.shape, jnp.float32)
     ext_rows = band + 2 * HALO
     return pl.pallas_call(
-        ptycho_kernel,
-        out_shape=(rim, jax.ShapeDtypeStruct(own.shape, jnp.float32), rim),
-        in_specs=[smem, smem] + [vmem] * 10,
-        out_specs=(vmem, vmem, vmem),
+        functools.partial(ptycho_kernel, own_blocks),
+        out_shape=(
+            rim, jax.ShapeDtypeStruct(own.shape, jnp.float32), rim,
+            jax.ShapeDtypeStruct((places,), jnp.int32),
+            jax.ShapeDtypeStruct((slots,), jnp.int32),
+            jax.ShapeDtypeStruct((places,), jnp.int32),
+            jax.ShapeDtypeStruct((places,), jnp.float32),
+            jax.ShapeDtypeStruct((slots,), jnp.float32),
+        ),
+        in_specs=[smem] * 4 + [vmem] * 10,
+        out_specs=(vmem, vmem, vmem) + (smem,) * 5,
         scratch_shapes=[
             pltpu.VMEM((2, NW // PC, ext_rows, PC), jnp.float32),
             pltpu.VMEM((2, NW // PC, ext_rows, PC), jnp.float32),
@@ -158,10 +335,7 @@
         cost_estimate=pl.CostEstimate(
             flops=2000000000, bytes_accessed=2000000, transcendentals=500000
         ),
-    )(rows, cols, before, own, after, measured, field, mask, *tables)
-
-
-MESH = pl.DeviceIdType.MESH
+    )(ids, counts, rows, cols, before, own, after, measured, field, mask, *tables)
 
 
 def tail_kernel(
@@ -415,43 +589,18 @@
     ray_counts,
     volume,
 ):
-    up, down = neighbours("tile")
-    band_rows = projection.shape[2]
-    before = lax.ppermute(projection[:, :, band_rows - HALO :], "tile", up)
-    after = lax.ppermute(projection[:, :, :HALO], "tile", down)
-    top, gradient, bottom = patch_sums(
-        before, projection, after, row_start, column_start, intensity, probe_field, probe_mask
+    groups = lax.axis_size("angle")
+    slot_count = ray_blocks.size
+    own_blocks = volume.shape[0]
+    capacity = max(2, -(-slot_count // groups))
+    before, after, ids = gather_head(projection, ray_blocks)
+    top, gradient, bottom, *scalars = patch_sums(
+        own_blocks, capacity, ids, ray_counts, before, projection, after, row_start, column_start,
+        intensity, probe_field, probe_mask
     )
-    angle_count = weights.shape[0]
-    own_blocks = volume.shape[0]
-    live = lax.iota(jnp.int32, CMAX)[None, None, :] < ray_counts[:, :, None]
-    groups = lax.axis_size("angle")
-    slot_count = angle_count * NRB * CMAX
-    capacity = max(2, -(-slot_count // groups))
-    flat_ids = ray_blocks.reshape(slot_count)
-    owners = flat_ids // own_blocks
-    local_ids = flat_ids % own_blocks
-    owner_hits = (owners[:, None] == lax.iota(jnp.int32, groups)[None, :]).astype(jnp.int32)
-    slot_ranks = jnp.sum((jnp.cumsum(owner_hits, axis=0) - 1) * owner_hits, axis=1)
-    slot_place = owners * capacity + slot_ranks
-    requests = (
-        jnp.zeros((groups * capacity,), jnp.int32)
-        .at[slot_place]
-        .set(local_ids)
-        .reshape(groups, capacity)
-    )
-    wanted = lax.all_to_all(requests, "angle", split_axis=0, concat_axis=0, tiled=True).reshape(
-        groups * capacity
-    )
-    places = lax.iota(jnp.int32, groups * capacity)
-    hits = (places[:, None] == slot_place[None, :]).astype(jnp.int32)
-    place_slot = jnp.sum(hits * lax.iota(jnp.int32, slot_count)[None, :], axis=1)
-    place_used = jnp.sum(hits, axis=1).astype(jnp.float32)
-    live_scale = live.reshape(slot_count).astype(jnp.float32)
-    scalars = (wanted, slot_place, place_slot, place_used, live_scale)
     tiles = weights.reshape(slot_count, RB, PIX)
     arrays = (top, gradient, bottom, projection, multiplier, reprojection, tiles, volume)
-    return finish(scalars, arrays, capacity)
+    return write_out(finish(scalars, arrays, capacity))
 
 
 def solution(mesh):

time: 66.2 us -> 53.6 us (0.81)
  Pallas kernels: 34.4 us -> 51.4 us
  starting transfers between devices: 13.2 us -> 0 us
  local copies, waits for them, and re-layouts: 10.7 us -> 1.27 us
  waiting for transfers between devices: 3.81 us -> 0 us
  other arithmetic: 2.96 us -> 0 us
    pallas_call x1 -> x3, Pallas kernels: 9.07 us -> 23.4 us  [the longest x1 11.5 us: gather_head(): pl.pallas_call(functools.partial(head_kernel, groups, tiles), out_shape=(...]
    all_to_all x1 -> x0, starting transfers between devices: 6.98 us -> none  [shards(): lax.all_to_all(requests, 'angle', split_axis=0, concat_axis=0, tiled=True)]
    ppermute x2 -> x0, starting transfers between devices: 6.17 us -> none  [the longest x1 4.88 us: shards(): before = lax.ppermute(projection[:, :, band_rows - HALO:], 'tile', up)]
    unnamed x9 -> x0, local copies, waits for them, and re-layouts: 6.08 us -> none
    all_to_all x1 -> x0, waiting for transfers between devices: 3.8 us -> none  [shards(): lax.all_to_all(requests, 'angle', split_axis=0, concat_axis=0, tiled=True)]
    pallas_call x1, Pallas kernels: 25.3 us -> 28 us  [finish(): pl.pallas_call(functools.partial(tail_kernel, groups, tiles, capacity), o...]
    convert_element_type x3 -> x0, other arithmetic: 1.4 us -> none  [the longest x1 0.75 us: shards(): live_scale = live.reshape(slot_count).astype(jnp.float32)]
    all_to_all x2 -> x0, local copies, waits for them, and re-layouts: 1.18 us -> none  [shards(): lax.all_to_all(requests, 'angle', split_axis=0, concat_axis=0, tiled=True)]
  transfers between devices with their start and end apart: 3 -> 0, of which waited for: 1 -> 0; matrix products, arithmetic and copies ran while one was open for 10% -> 0% of each run, Pallas kernels for 0% -> 0%
where the time goes in v3:
time: 53.6 us; the launch traced here: 53.3 us
  Pallas kernels  51.4 us (96%)
  local copies, waits for them, and re-layouts  1.27 us (2%)
  between operations  0.65 us (1%)
    pallas_call x1, Pallas kernels, finish(): pl.pallas_call(functools.partial(tail_kernel, groups, tiles, capacity), o...  28 us
    pallas_call x1, Pallas kernels, gather_head(): pl.pallas_call(functools.partial(head_kernel, groups, tiles), out_shape=(...  11.5 us
    pallas_call x1, Pallas kernels, patch_sums(): pl.pallas_call(functools.partial(ptycho_kernel, own_blocks), out_shape=(r...  10.1 us
    pallas_call x1, Pallas kernels, write_out(): pl.pallas_call(write_kernel, out_shape=tuple((jax.ShapeDtypeStruct(v.shap...  1.89 us
    reshape x1, local copies, waits for them, and re-layouts, gather_head(): ray_blocks.reshape(1, slots)  1.27 us

profile of v3, /device:TPU:0, one launch (start us, length us, event | category | flops | bytes accessed | tf_op | source)
XLA Modules:
  0.0 53.3 jit_solution(1079999229486433983)
XLA Ops:
  0.6 1.3 %reshape.12.ids_ref = s32[1,16]{1,0:T(1,128)} reshape(s32[2,2,4]{2,1,0:T(2,128)} %param.25) | data formatting | bytes 128 | tf_op jit(solution)/shard_map/reshape | solution.py:144
  1.9 11.5 %shard_map.175 = (f32[1,2,32,256]{3,2,1,0:T(8,128)}, f32[1,2,32,256]{3,2,1,0:T(8,128)}, s32[8,1,16]{2,1,0:T(1,128)}) custom-call(f32[1,2,32,256]{3,2,1,0:T(8,128)} %proj_ref.3, s32[1,16]{1,0:T(1,128)} %reshape.12.ids_ref), custom_call_target="tpu_custom_call" | custom-call | tf_op jit(solution)/shard_map/pallas_call | solution.py:132
  13.4 10.1 %shard_map.176 = (f32[1,2,32,256]{3,2,1,0:T(8,128)}, f32[1,2,32,256]{3,2,1,0:T(8,128)}, f32[1,2,32,256]{3,2,1,0:T(8,128)}, s32[16]{0:T(128)}, s32[16]{0:T(128)},...) custom-call(s32[8,1,16]{2,1,0:T(1,128)} %get-tuple-element.17.all_ref, s32[2,2]{1,0:T(2,128)} %counts_ref.1, s32[1,32]{1,0:T(1,128)} %rows_ref.1, ...), custom_call_target="tpu_custom_call" | custom-call | flops 2000000000 | bytes 2000000 | tf_op jit(solution)/shard_map/pallas_call | solution.py:318
  23.4 28.0 %shard_map.177 = (f32[1,2,32,256]{3,2,1,0:T(8,128)}, f32[16,16,512]{2,1,0:T(8,128)}, f32[2,2,16,256]{3,2,1,0:T(8,128)}) custom-call(s32[16]{0:T(128)} %get-tuple-element.20.wanted_ref, s32[16]{0:T(128)} %get-tuple-element.21.place_ref, s32[16]{0:T(128)} %get-tuple-element.22.slot_ref, f32[16]{0:T(128)} %get-tuple-element.23.used_ref, ...), custom_call_target="tpu_custom_call" | custom-call | tf_op jit(solution)/shard_map/pallas_call | solution.py:551
  51.4 1.9 %shard_map.178 = (f32[1,2,32,256]{3,2,1,0:T(8,128)}, f32[16,16,512]{2,1,0:T(8,128)}, f32[2,2,16,256]{3,2,1,0:T(8,128)}) custom-call(f32[1,2,32,256]{3,2,1,0:T(8,128)} %get-tuple-element.28.a_ref, f32[16,16,512]{2,1,0:T(8,128)} %get-tuple-element.29.b_ref, f32[2,2,16,256]{3,2,1,0:T(8,128)} %get-tuple-element.30.c_ref), custom_call_target="tpu_custom_call" | custom-call | tf_op jit(solution)/shard_map/pallas_call | solution.py:201

commit v4 on v1

v4 whole, which is shorter than its diff:
```python
import functools

import jax
import jax.numpy as jnp
import numpy as np
from jax import lax
from jax.experimental import pallas as pl
from jax.experimental.pallas import tpu as pltpu
from jax.sharding import PartitionSpec as P

PR = 64
PC = 128
NW = 256
PIX = 512
RB = 128
CMAX = 4
HALO = 32
NRB = 2


penalty = 0.5
descent = 0.25
volume_step = 1.0
damping = 0.1


def dft_blocks(sign):
    def table(length):
        counter = np.arange(length)
        phase = (counter[:, None] * counter[None, :] % length) * (2.0 * np.pi / length)
        return np.cos(phase) / np.sqrt(length), sign * np.sin(phase) / np.sqrt(length)

    row_cos, row_sin = table(PR)
    col_cos, col_sin = table(PC)
    left = np.block([[row_cos, -row_sin], [row_sin, row_cos]])
    right = np.block([[col_cos, col_sin], [-col_sin, col_cos]])
    return left.astype(np.float32), right.astype(np.float32)


MESH = pl.DeviceIdType.MESH
CHUNK = 4


def step_kernel(
    groups, tiles, capacity,
    mine_ref, counts_ref, rows_ref, cols_ref,
    ids_ref, proj_ref, mult_ref, prior_ref, measured_ref, field_ref, mask_ref,
    left_f_ref, right_f_ref, left_b_ref, right_b_ref, vol_ref, weight_hbm,
    updated_ref, new_vol_ref, new_mult_ref,
    all_ref, all_smem, wanted_ref, place_ref, slot_ref, used_ref, live_ref,
    weight_ref, before_ref, after_ref, above_ref, below_ref,
    ext_ref, acc_ref, wave_ref, stage_ref,
    moved_ref, mult_moved_ref, half_send_ref,
    send_a, send_b, send_c, recv_a, recv_b, recv_c, spread_ref, wide_ref,
    send_sem, recv_sem, near_send, near_recv, local_sem,
):
    g = lax.axis_index("angle")
    t = lax.axis_index("tile")
    h = lax.axis_index("half")
    band = proj_ref.shape[2]
    part = band // 2
    places = groups * capacity
    own_blocks = vol_ref.shape[0]
    angles, blocks, per_block = mine_ref.shape
    slots = angles * blocks * per_block
    has_up = t > 0
    has_down = t < tiles - 1
    half = jnp.bfloat16
    sends = (send_a, send_b, send_c)
    recvs = (recv_a, recv_b, recv_c)
    lanes = [slice(0, PC), slice(PC, NW)]

    def where_of(slot):
        pair, c = divmod(slot, per_block)
        angle, block = divmod(pair, blocks)
        return angle, block, c

    barrier = pltpu.get_barrier_semaphore()

    def greet(where):
        pl.semaphore_signal(barrier, inc=1, device_id=where, device_id_type=MESH)

    for d in range(1, groups):
        greet({"angle": lax.rem(g + d, groups)})
    greet({"half": 1 - h})

    @pl.when(has_up)
    def _():
        greet({"tile": t - 1})

    @pl.when(has_down)
    def _():
        greet({"tile": t + 1})

    weight_copy = pltpu.make_async_copy(weight_hbm, weight_ref, local_sem.at[0])
    weight_copy.start()

    owners = [lax.div(mine_ref[where_of(s)], own_blocks) for s in range(slots)]
    my_places = []
    for s in range(slots):
        rank = jnp.int32(0)
        for earlier in range(s):
            rank = rank + jnp.where(owners[earlier] == owners[s], 1, 0)
        my_places.append(owners[s] * capacity + rank)
        place_ref[s] = my_places[s]
        angle, block, c = where_of(s)
        live_ref[s] = jnp.where(c < counts_ref[angle, block], 1.0, 0.0)

    def slot_of(n, carry):
        slot = jnp.int32(0)
        used = jnp.float32(0.0)
        for s in range(slots):
            hit = place_ref[s] == n
            slot = jnp.where(hit, s, slot)
            used = jnp.where(hit, 1.0, used)
        slot_ref[n] = slot
        used_ref[n] = used
        return carry

    pl.semaphore_wait(barrier, groups + has_up.astype(jnp.int32) + has_down.astype(jnp.int32))

    def angle_copy(phase, d, source, target):
        return pltpu.make_async_remote_copy(
            src_ref=source,
            dst_ref=target,
            send_sem=send_sem.at[phase, d],
            recv_sem=recv_sem.at[phase, d],
            device_id={"angle": lax.rem(g + d, groups)},
            device_id_type=MESH,
        )

    id_copies = [angle_copy(3, d, ids_ref, all_ref.at[g]) for d in range(1, groups)]
    for copy in id_copies:
        copy.start()

    def exchange(phase):
        copies = []
        for d in range(1, groups):
            peer = lax.rem(g + d, groups)
            copies.append(
                angle_copy(
                    phase, d,
                    sends[phase].at[pl.ds(peer * capacity, capacity)],
                    recvs[phase].at[pl.ds(g * capacity, capacity)],
                )
            )
            copies[-1].start()
        own = pl.ds(g * capacity, capacity)
        recvs[phase][own] = sends[phase][own]
        return copies

    def near(index, source, target, where):
        return pltpu.make_async_remote_copy(
            src_ref=source,
            dst_ref=target,
            send_sem=near_send.at[index],
            recv_sem=near_recv.at[index],
            device_id=where,
            device_id_type=MESH,
        )

    def to_tiles(index, down_source, down_target, up_source, up_target):
        down = near(index, down_source, down_target, {"tile": jnp.minimum(t + 1, tiles - 1)})
        up = near(index + 1, up_source, up_target, {"tile": jnp.maximum(t - 1, 0)})

        @pl.when(has_down)
        def _():
            down.start()

        @pl.when(has_up)
        def _():
            up.start()

        @pl.when(jnp.logical_not(has_up))
        def _():
            down_target[...] = jnp.zeros_like(down_target)

        @pl.when(jnp.logical_not(has_down))
        def _():
            up_target[...] = jnp.zeros_like(up_target)

        return down, up

    def from_tiles(down, up):
        @pl.when(has_up)
        def _():
            down.wait_recv()

        @pl.when(has_down)
        def _():
            up.wait_recv()

    def sent_to_tiles(down, up):
        @pl.when(has_down)
        def _():
            down.wait_send()

        @pl.when(has_up)
        def _():
            up.wait_send()

    halo = to_tiles(
        0, proj_ref.at[0, :, band - HALO :, :], before_ref, proj_ref.at[0, :, :HALO, :], after_ref
    )
    away = pl.ds(pl.multiple_of((1 - h) * part, part), part)
    here = pl.ds(pl.multiple_of(h * part, part), part)
    mult_copy = near(4, mult_ref.at[0, :, away, :], mult_moved_ref.at[h], {"half": 1 - h})
    mult_copy.start()
    mult_moved_ref[h] = mult_ref[0, :, here, :]
    all_ref[g] = ids_ref[...]
    lax.fori_loop(0, places, slot_of, 0)
    for side in range(2):
        ext_ref[:, side, HALO : HALO + band] = proj_ref[0, :, :, lanes[side]]
    acc_ref[...] = jnp.zeros_like(acc_ref)
    stage_ref[...] = jnp.zeros_like(stage_ref)
    mask = mask_ref[...].astype(jnp.float32)
    wave_ref[0] = field_ref[0] * mask
    wave_ref[1] = field_ref[1] * mask

    for copy in id_copies:
        copy.wait_recv()
    id_local = pltpu.make_async_copy(all_ref, all_smem, local_sem.at[1])
    id_local.start()
    id_local.wait()

    def group(peer, carry):
        found = jnp.int32(0)
        values = [jnp.int32(0)] * capacity
        for s in range(slots):
            b = all_smem[(peer,) + where_of(s)]
            hit = lax.div(b, own_blocks) == g
            inside = lax.rem(b, own_blocks)
            values = [
                jnp.where(jnp.logical_and(hit, found == r), inside, values[r])
                for r in range(capacity)
            ]
            found = found + jnp.where(hit, 1, 0)
        for r in range(capacity):
            wanted_ref[peer * capacity + r] = values[r]
        return carry

    lax.fori_loop(0, groups, group, 0)
    for n in range(places):
        send_a[n] = vol_ref[wanted_ref[n]].astype(half)
    fetches = exchange(0)
    from_tiles(*halo)
    for side in range(2):
        ext_ref[:, side, :HALO] = before_ref[:, :, lanes[side]]
        ext_ref[:, side, HALO + band :] = after_ref[:, :, lanes[side]]

    lane = lax.broadcasted_iota(jnp.int32, (PR, PC), 1)
    ext_rows = band + 2 * HALO
    wide_lane = lax.broadcasted_iota(jnp.int32, (ext_rows, PC), 1)

    def dot(a, b):
        return jnp.dot(a, b, preferred_element_type=jnp.float32)

    def step(chunk, carry):
        waves = []
        spots = []
        for j in range(CHUNK):
            p = chunk * CHUNK + j
            row = rows_ref[0, p] + HALO
            col = cols_ref[0, p]
            spots.append((row, col))
            back_shift = lax.rem(NW - col, PC)

            def window(channel):
                near = pltpu.roll(ext_ref[channel, 0, pl.ds(row, PR), :], back_shift, 1)
                next_ = pltpu.roll(ext_ref[channel, 1, pl.ds(row, PR), :], back_shift, 1)
                return jnp.where(lane + col < PC, near, next_)

            o_re = window(0)
            o_im = window(1)
            p_re, p_im = wave_ref[0], wave_ref[1]
            waves.append(
                jnp.concatenate([p_re * o_re - p_im * o_im, p_re * o_im + p_im * o_re], axis=0)
            )
        wide = jnp.concatenate(waves, axis=1).astype(half)
        first = dot(left_f_ref[...], wide).astype(half)
        tall = jnp.concatenate(
            [
                jnp.concatenate(
                    [first[:PR, j * PC : (j + 1) * PC], first[PR:, j * PC : (j + 1) * PC]], axis=1
                )
                for j in range(CHUNK)
            ],
            axis=0,
        )
        far = dot(tall, right_f_ref[...])
        f_re, f_im = far[:, :PC], far[:, PC:]
        measured = measured_ref[0, pl.ds(chunk * CHUNK, CHUNK)].astype(jnp.float32)
        measured = measured.reshape(CHUNK * PR, PC)
        factor = 1.0 - jnp.sqrt(measured) * lax.rsqrt(f_re * f_re + f_im * f_im + 1.0)
        scaled = jnp.concatenate([f_re * factor, f_im * factor], axis=1).astype(half)
        second = dot(scaled, right_b_ref[...]).astype(half)
        wide = jnp.concatenate(
            [
                jnp.concatenate(
                    [second[j * PR : (j + 1) * PR, :PC], second[j * PR : (j + 1) * PR, PC:]], axis=0
                )
                for j in range(CHUNK)
            ],
            axis=1,
        )
        back = dot(left_b_ref[...], wide)
        above = ext_rows - PR
        for j in range(CHUNK):
            shift = lax.rem(spots[j][1], PC)
            b_re = back[:PR, j * PC : (j + 1) * PC]
            b_im = back[PR:, j * PC : (j + 1) * PC]
            p_re, p_im = wave_ref[0], wave_ref[1]
            stage_ref[j, 0, above : above + PR] = pltpu.roll(p_re * b_re + p_im * b_im, shift, 1)
            stage_ref[j, 1, above : above + PR] = pltpu.roll(p_re * b_im - p_im * b_re, shift, 1)
        for channel in range(2):
            first_half = acc_ref[channel, 0]
            next_half = acc_ref[channel, 1]
            for j in range(CHUNK):
                row, col = spots[j]
                values = stage_ref[j, channel, pl.ds(above - row, ext_rows), :]
                first_half = first_half + jnp.where(wide_lane >= col, values, 0.0)
                next_half = next_half + jnp.where(wide_lane >= col, 0.0, values)
            acc_ref[channel, 0] = first_half
            acc_ref[channel, 1] = next_half
        return carry

    lax.fori_loop(0, rows_ref.shape[1] // CHUNK, step, 0)
    rims = to_tiles(
        2, acc_ref.at[:, :, HALO + band :, :], above_ref, acc_ref.at[:, :, :HALO, :], below_ref
    )
    from_tiles(*rims)
    for side in range(2):
        for channel in range(2):
            gradient = acc_ref[channel, side, HALO : HALO + band]
            above = above_ref[channel, side]
            below = below_ref[channel, side]
            if band == HALO:
                gradient = gradient + above + below
            else:
                still = jnp.zeros((band - HALO, PC), jnp.float32)
                gradient = gradient + jnp.concatenate([above, still], axis=0)
                gradient = gradient + jnp.concatenate([still, below], axis=0)
            old = proj_ref[0, channel, :, lanes[side]]
            held = 1.0 if channel == 0 else prior_ref[0, :, lanes[side]]
            updated_ref[0, channel, :, lanes[side]] = old - descent * (
                gradient + penalty * (old - held) + mult_ref[0, channel, :, lanes[side]]
            )
    half_send_ref[...] = updated_ref[0, :, away, :]
    moved_copy = near(5, half_send_ref, moved_ref.at[h], {"half": 1 - h})
    moved_copy.start()
    moved_ref[h] = updated_ref[0, :, here, :]
    for copy in fetches:
        copy.wait_recv()
    mult_copy.wait_recv()
    weight_copy.wait()

    def projected(phase, pair):
        total = jnp.zeros((part, RB), jnp.float32)
        for c in range(per_block):
            slot = pair * per_block + c
            picked = recvs[phase][place_ref[slot]]
            total = total + live_ref[slot] * lax.dot_general(
                picked, weight_ref[where_of(slot)], (((1,), (1,)), ((), ())),
                preferred_element_type=jnp.float32,
            )
        return total

    pairs = slots // per_block
    sinos = [projected(0, pair) for pair in range(pairs)]
    moved_copy.wait_recv()
    for pair in range(pairs):
        angle, k = divmod(pair, NRB)
        rays = slice(k * RB, (k + 1) * RB)
        target = moved_ref[angle, 1, :, rays] + mult_moved_ref[angle, 1, :, rays] / penalty
        residual = (sinos[pair] - target).astype(half)
        for c in range(per_block):
            slot = pair * per_block + c
            spread = live_ref[slot] * jnp.dot(
                residual, weight_ref[where_of(slot)], preferred_element_type=jnp.float32
            )
            spread_ref[slot] = spread.astype(half)
    for n in range(places):
        send_b[n] = spread_ref[slot_ref[n]] * used_ref[n].astype(half)
    terms = exchange(1)
    for copy in terms:
        copy.wait_recv()
    for n in range(places):
        wide_ref[n] = recv_b[n].astype(jnp.float32)

    def renew(j, carry):
        total = jnp.zeros(wide_ref.shape[1:], jnp.float32)
        for n in range(places):
            total = total + jnp.where(wanted_ref[n] == j, 1.0, 0.0) * wide_ref[n]
        block = vol_ref[j]
        new_vol_ref[j] = block - volume_step * (total + damping * block)
        return carry

    lax.fori_loop(0, own_blocks, renew, 0)
    for n in range(places):
        send_c[n] = new_vol_ref[wanted_ref[n]].astype(half)
    renewals = exchange(2)
    for angle in range(moved_ref.shape[0]):
        new_mult_ref[angle, 0] = mult_moved_ref[angle, 0] + penalty * (moved_ref[angle, 0] - 1.0)
    for copy in renewals:
        copy.wait_recv()
    for pair in range(pairs):
        angle, k = divmod(pair, NRB)
        rays = slice(k * RB, (k + 1) * RB)
        fresh = projected(2, pair)
        new_mult_ref[angle, 1, :, rays] = mult_moved_ref[angle, 1, :, rays] + penalty * (
            moved_ref[angle, 1, :, rays] - fresh
        )
    for copy in id_copies + fetches + terms + renewals + [mult_copy, moved_copy]:
        copy.wait_send()
    sent_to_tiles(*halo)
    sent_to_tiles(*rims)


def admm_step(ray_blocks, counts, rows, cols, own, multiplier, prior, measured, field, mask, volume, weights):
    groups = lax.axis_size("angle")
    tiles = lax.axis_size("tile")
    slots = ray_blocks.size
    capacity = max(2, -(-slots // groups))
    places = groups * capacity
    left_f, right_f = dft_blocks(-1.0)
    left_b, right_b = dft_blocks(1.0)
    tables = [jnp.asarray(m, jnp.bfloat16) for m in (left_f, right_f, left_b, right_b)]
    vmem = pl.BlockSpec(memory_space=pltpu.VMEM)
    smem = pl.BlockSpec(memory_space=pltpu.SMEM)
    band = own.shape[2]
    ext_rows = band + 2 * HALO
    block = volume.shape[1:]
    moved_shape = (2, 2, band // 2, NW)
    ids = (groups,) + ray_blocks.shape
    f32 = jnp.float32
    return pl.pallas_call(
        functools.partial(step_kernel, groups, tiles, capacity),
        out_shape=(
            jax.ShapeDtypeStruct(own.shape, f32),
            jax.ShapeDtypeStruct(volume.shape, f32),
            jax.ShapeDtypeStruct(moved_shape, f32),
        ),
        in_specs=[smem] * 4 + [vmem] * 12 + [pl.BlockSpec(memory_space=pl.ANY)],
        out_specs=(vmem, vmem, vmem),
        scratch_shapes=[
            pltpu.VMEM(ids, jnp.int32),
            pltpu.SMEM(ids, jnp.int32),
            pltpu.SMEM((places,), jnp.int32),
            pltpu.SMEM((slots,), jnp.int32),
            pltpu.SMEM((places,), jnp.int32),
            pltpu.SMEM((places,), f32),
            pltpu.SMEM((slots,), f32),
            pltpu.VMEM(weights.shape, jnp.bfloat16),
            pltpu.VMEM((2, HALO, NW), f32),
            pltpu.VMEM((2, HALO, NW), f32),
            pltpu.VMEM((2, NW // PC, HALO, PC), f32),
            pltpu.VMEM((2, NW // PC, HALO, PC), f32),
            pltpu.VMEM((2, NW // PC, ext_rows, PC), f32),
            pltpu.VMEM((2, NW // PC, ext_rows, PC), f32),
            pltpu.VMEM((2, PR, PC), f32),
            pltpu.VMEM((CHUNK, 2, 2 * (ext_rows - PR) + PR, PC), f32),
            pltpu.VMEM(moved_shape, f32),
            pltpu.VMEM(moved_shape, f32),
            pltpu.VMEM(moved_shape[1:], f32),
            *[pltpu.VMEM((places,) + block, jnp.bfloat16)] * 6,
            pltpu.VMEM((slots,) + block, jnp.bfloat16),
            pltpu.VMEM((places,) + block, f32),
            pltpu.SemaphoreType.DMA((4, groups)),
            pltpu.SemaphoreType.DMA((4, groups)),
            pltpu.SemaphoreType.DMA((6,)),
            pltpu.SemaphoreType.DMA((6,)),
            pltpu.SemaphoreType.DMA((2,)),
        ],
        compiler_params=pltpu.CompilerParams(collective_id=1, has_side_effects=True),
    )(
        ray_blocks, counts, rows, cols,
        ray_blocks, own, multiplier, prior, measured, field, mask, *tables, volume, weights,
    )


def write_kernel(a_ref, b_ref, c_ref, a_out, b_out, c_out, sems):
    copies = [
        pltpu.make_async_copy(source, target, sems.at[i])
        for i, (source, target) in enumerate(((a_ref, a_out), (b_ref, b_out), (c_ref, c_out)))
    ]
    for copy in copies:
        copy.start()
    for copy in copies:
        copy.wait()


def write_out(values):
    return pl.pallas_call(
        write_kernel,
        out_shape=tuple(jax.ShapeDtypeStruct(v.shape, v.dtype) for v in values),
        in_specs=[pl.BlockSpec(memory_space=pltpu.VMEM)] * 3,
        out_specs=tuple([pl.BlockSpec(memory_space=pl.ANY)] * 3),
        scratch_shapes=[pltpu.SemaphoreType.DMA((3,))],
    )(*values)


def shards(
    projection,
    multiplier,
    reprojection,
    intensity,
    row_start,
    column_start,
    probe_field,
    probe_mask,
    weights,
    ray_blocks,
    ray_counts,
    volume,
):
    return write_out(
        admm_step(
            ray_blocks, ray_counts, row_start, column_start, projection, multiplier, reprojection,
            intensity, probe_field, probe_mask, volume, weights,
        )
    )


def solution(mesh):
    return jax.shard_map(
        shards,
        mesh=mesh,
        in_specs=(
            P(("angle", "half"), None, "tile", None),
            P(("angle", "half"), None, "tile", None),
            P(("angle", "half"), "tile", None),
            P(("angle", "half"), "tile", None, None),
            P(("angle", "half"), "tile"),
            P(("angle", "half"), "tile"),
            P(),
            P(),
            P("angle", None, None, None, None),
            P("angle", None, None),
            P("angle", None),
            P("angle", ("tile", "half"), None),
        ),
        out_specs=(
            P(("angle", "half"), None, "tile", None),
            P("angle", ("tile", "half"), None),
            P("angle", None, ("tile", "half"), None),
        ),
        check_vma=False,
    )
```

time: 82.6 us -> 44.5 us (0.54)
  Pallas kernels: 9.08 us -> 43.6 us
  starting transfers between devices: 26.4 us -> 0 us
  waiting for transfers between devices: 25.7 us -> 0 us
  local copies, waits for them, and re-layouts: 12.3 us -> 0 us
  other arithmetic: 5.23 us -> 0 us
  matrix products: 2.05 us -> 0 us
    pallas_call x1 -> x2, Pallas kernels: 9.08 us -> 43.6 us  [the longest x1 41.7 us: admm_step(): pl.pallas_call(functools.partial(step_kernel, groups, tiles, capacity), o...]
    all_to_all x4 -> x0, waiting for transfers between devices: 24.2 us -> none  [the longest x2 13.2 us: fetch_blocks(): lax.all_to_all(replies, 'angle', split_axis=0, concat_axis=0, tiled=True)]
    all_to_all x4 -> x0, starting transfers between devices: 17.5 us -> none  [the longest x1 6.98 us: shards(): lax.all_to_all(requests, 'angle', split_axis=0, concat_axis=0, tiled=True)]
    ppermute x6 -> x0, starting transfers between devices: 8.95 us -> none  [the longest x1 4.88 us: shards(): before = lax.ppermute(projection[:, :, band_rows - HALO:], 'tile', up)]
    gather x4 -> x0, local copies, waits for them, and re-layouts: 3.64 us -> none  [the longest x2 2.52 us: fetch_blocks(): field.astype(jnp.bfloat16)[wanted]]
    unnamed x25 -> x0, local copies, waits for them, and re-layouts: 2.4 us -> none
    dot_general x3 -> x0, matrix products: 2.05 us -> none  [the longest x1 0.97 us: shards(): jnp.einsum('tkcrp,tskr->tkcsp', weights, residual, preferred_element_type...]
    convert_element_type x4 -> x0, other arithmetic: 1.93 us -> none  [the longest x1 1.07 us: fetch_blocks(): field.astype(jnp.bfloat16)[wanted]]
  transfers between devices with their start and end apart: 10 -> 0, of which waited for: 6 -> 0; matrix products, arithmetic and copies ran while one was open for 12% -> 0% of each run, Pallas kernels for 11% -> 0%
where the time goes in v4:
time: 44.5 us; the launch traced here: 44.3 us
  Pallas kernels  43.6 us (98%)
  between operations  0.64 us (1%)
    pallas_call x1, Pallas kernels, admm_step(): pl.pallas_call(functools.partial(step_kernel, groups, tiles, capacity), o...  41.7 us
    pallas_call x1, Pallas kernels, write_out(): pl.pallas_call(write_kernel, out_shape=tuple((jax.ShapeDtypeStruct(v.shap...  1.89 us

profile of v4, /device:TPU:0, one launch (start us, length us, event | category | flops | bytes accessed | tf_op | source)
XLA Modules:
  0.0 44.3 jit_solution(6334337541368620772)
XLA Ops:
  0.6 41.7 %shard_map.175 = (f32[1,2,32,256]{3,2,1,0:T(8,128)}, f32[16,16,512]{2,1,0:T(8,128)}, f32[2,2,16,256]{3,2,1,0:T(8,128)}) custom-call(s32[2,2,4]{2,1,0:T(2,128)} %ids_ref.1, s32[2,2]{1,0:T(2,128)} %counts_ref.1, s32[1,32]{1,0:T(1,128)} %rows_ref.1, s32[1,32]{1,0:T(1,128)} %cols_ref.1, s32[2,2,4]{2,1,0:T(2,128)} %ids_ref.1, f32[1,2,32,256]{3,2,1,0:T(8,128)} %proj_ref.1, ...), custom_call_target="tpu_custom_call" | custom-call | tf_op jit(solution)/shard_map/pallas_call | solution.py:436
  42.4 1.9 %shard_map.176 = (f32[1,2,32,256]{3,2,1,0:T(8,128)}, f32[16,16,512]{2,1,0:T(8,128)}, f32[2,2,16,256]{3,2,1,0:T(8,128)}) custom-call(f32[1,2,32,256]{3,2,1,0:T(8,128)} %get-tuple-element.6.a_ref, f32[16,16,512]{2,1,0:T(8,128)} %get-tuple-element.7.b_ref, f32[2,2,16,256]{3,2,1,0:T(8,128)} %get-tuple-element.8.c_ref), custom_call_target="tpu_custom_call" | custom-call | tf_op jit(solution)/shard_map/pallas_call | solution.py:493

commit v5 on v4

--- a/solution.py
+++ b/solution.py
@@ -37,8 +37,14 @@
     return left.astype(np.float32), right.astype(np.float32)
 
 
+def split_table(matrix):
+    coarse = matrix.astype(jnp.bfloat16)
+    rest = (matrix - coarse.astype(np.float32)).astype(jnp.bfloat16)
+    return jnp.asarray(np.concatenate([coarse, rest], axis=1))
+
+
 MESH = pl.DeviceIdType.MESH
-CHUNK = 4
+CHUNK = 16
 
 
 def step_kernel(
@@ -277,7 +283,7 @@
                 jnp.concatenate([p_re * o_re - p_im * o_im, p_re * o_im + p_im * o_re], axis=0)
             )
         wide = jnp.concatenate(waves, axis=1).astype(half)
-        first = dot(left_f_ref[...], wide).astype(half)
+        first = dot(left_f_ref[...], jnp.concatenate([wide, wide], axis=0)).astype(half)
         tall = jnp.concatenate(
             [
                 jnp.concatenate(
@@ -303,7 +309,7 @@
             ],
             axis=1,
         )
-        back = dot(left_b_ref[...], wide)
+        back = dot(left_b_ref[...], jnp.concatenate([wide, wide], axis=0))
         above = ext_rows - PR
         for j in range(CHUNK):
             shift = lax.rem(spots[j][1], PC)
@@ -424,7 +430,8 @@
     places = groups * capacity
     left_f, right_f = dft_blocks(-1.0)
     left_b, right_b = dft_blocks(1.0)
-    tables = [jnp.asarray(m, jnp.bfloat16) for m in (left_f, right_f, left_b, right_b)]
+    left_f, left_b = (split_table(m) for m in (left_f, left_b))
+    tables = [left_f, jnp.asarray(right_f, jnp.bfloat16), left_b, jnp.asarray(right_b, jnp.bfloat16)]
     vmem = pl.BlockSpec(memory_space=pltpu.VMEM)
     smem = pl.BlockSpec(memory_space=pltpu.SMEM)
     band = own.shape[2]

time: 44.5 us -> 40.3 us (0.906)
  Pallas kernels: 43.6 us -> 39.5 us
    pallas_call x1, Pallas kernels: 41.7 us -> 37.6 us  [admm_step(): pl.pallas_call(functools.partial(step_kernel, groups, tiles, capacity), o...]
where the time goes in v5:
time: 40.3 us; the launch traced here: 40.1 us
  Pallas kernels  39.5 us (98%)
  between operations  0.64 us (2%)
    pallas_call x1, Pallas kernels, admm_step(): pl.pallas_call(functools.partial(step_kernel, groups, tiles, capacity), o...  37.6 us
    pallas_call x1, Pallas kernels, write_out(): pl.pallas_call(write_kernel, out_shape=tuple((jax.ShapeDtypeStruct(v.shap...  1.89 us

profile of v5, /device:TPU:0, one launch (start us, length us, event | category | flops | bytes accessed | tf_op | source)
XLA Modules:
  0.0 40.1 jit_solution(2346384347163550304)
XLA Ops:
  0.6 37.6 %shard_map.175 = (f32[1,2,32,256]{3,2,1,0:T(8,128)}, f32[16,16,512]{2,1,0:T(8,128)}, f32[2,2,16,256]{3,2,1,0:T(8,128)}) custom-call(s32[2,2,4]{2,1,0:T(2,128)} %ids_ref.1, s32[2,2]{1,0:T(2,128)} %counts_ref.1, s32[1,32]{1,0:T(1,128)} %rows_ref.1, s32[1,32]{1,0:T(1,128)} %cols_ref.1, s32[2,2,4]{2,1,0:T(2,128)} %ids_ref.1, f32[1,2,32,256]{3,2,1,0:T(8,128)} %proj_ref.1, ...), custom_call_target="tpu_custom_call" | custom-call | tf_op jit(solution)/shard_map/pallas_call | solution.py:443
  38.3 1.9 %shard_map.176 = (f32[1,2,32,256]{3,2,1,0:T(8,128)}, f32[16,16,512]{2,1,0:T(8,128)}, f32[2,2,16,256]{3,2,1,0:T(8,128)}) custom-call(f32[1,2,32,256]{3,2,1,0:T(8,128)} %get-tuple-element.6.a_ref, f32[16,16,512]{2,1,0:T(8,128)} %get-tuple-element.7.b_ref, f32[2,2,16,256]{3,2,1,0:T(8,128)} %get-tuple-element.8.c_ref), custom_call_target="tpu_custom_call" | custom-call | tf_op jit(solution)/shard_map/pallas_call | solution.py:500
